TPU v7x, 32 devices: a whole 2x2x4 slice. The times are simulated.
32 devices in a mesh: groups: 2 (over y), gx: 4 (over z), gy: 2 (over x), gz: 2 (over core).
Axes of the slice: x: 2, y: 2, z: 4, core: 2. Of those that a mesh axis runs over, the one named last changes fastest.
Arguments:
- polar_angle: float32 [16, 512, 256], P('gz', ('groups', 'gx'), 'gy'), parts along dimension 1, may hold values from -3.140625 to 3.140625
- azimuth: float32 [16, 512, 256], P('gz', ('groups', 'gx'), 'gy'), parts along dimension 1, may hold values from -3.140625 to 3.140625
- classes: int32 [6, 16, 512, 256], P(None, 'gz', ('groups', 'gx'), 'gy'), parts along dimension 2, may hold values from 0 to 7, as said below
- exchange_table: float32 [8], replicated, may hold values from 0.3 to 1.5
Outputs:
- spins_final: float32 [3, 16, 512, 256], P(None, 'gz', ('groups', 'gx'), 'gy'), parts along dimension 2
- modes_mid: float32 [32, 6144], P(('groups', 'gx')), parts along dimension 0
- modes_end: float32 [32, 6144], P(('groups', 'gx')), parts along dimension 0
There are 2 independent parts, one for each index of `groups`. A program takes and returns all parts, laid end to end along the dimension named above; an argument that names none is the same for every part. Nothing has to cross between parts.
Inputs may be any that keep to these rules, and one draw needn't show every extreme that they name: `classes`: entry 3 + d of a site equals entry d of its lower neighbour along direction d (periodically), so every bond has one class seen from both ends.
All inputs are finite; a program needn't handle non-finite values.
Results may differ from a plain program's by a relative error of at most 0.0001.
Values sent between devices are 32-bit elements; how exact they have to be, the bound alone decides.
A program may use at most 128 MiB of HBM per device.

v0:
```python
import functools
import math

import jax
import jax.numpy as jnp
import numpy as np
from jax import lax
from jax.experimental import pallas as pl
from jax.experimental.pallas import tpu as pltpu
from jax.sharding import PartitionSpec as P

KX = 32
KY = 32
STEPS = 4
HALO = 8
MESH = pl.DeviceIdType.MESH

time_step = 0.1
damping = 0.1


def sin_cos(angle):
    turns = jnp.floor(angle * (2.0 / math.pi) + 0.5)
    rest = angle - turns * 1.5703125
    rest = rest - turns * 4.837512969970703125e-4
    rest = rest - turns * 7.54978995489188216e-8
    square = rest * rest
    sine = rest + rest * square * (
        -1.6666654611e-1 + square * (8.3321608736e-3 + square * -1.9515295891e-4)
    )
    cosine = (1.0 - 0.5 * square) + square * square * (
        4.166664568298827e-2 + square * (-1.388731625493765e-3 + square * 2.443315711809948e-5)
    )
    size = jnp.abs(turns)
    odd = size == 1.0
    half = size == 2.0
    sine_out = jnp.where(odd, jnp.where(turns > 0.0, cosine, -cosine), jnp.where(half, -sine, sine))
    cosine_out = jnp.where(odd, jnp.where(turns > 0.0, -sine, sine), jnp.where(half, -cosine, cosine))
    return sine_out, cosine_out


def spins_of(polar, azimuth):
    sine_polar, cosine_polar = sin_cos(polar)
    sine_azimuth, cosine_azimuth = sin_cos(azimuth)
    return sine_polar * cosine_azimuth, sine_polar * sine_azimuth, cosine_polar


def lookup(classes, table_ref):
    values = [table_ref[i] for i in range(table_ref.shape[0])]
    bit = 1
    level = None
    while len(values) > 1:
        mask = (classes & bit) != 0
        values = [
            jnp.where(mask, values[i + 1], values[i]) if i + 1 < len(values) else values[i]
            for i in range(0, len(values), 2)
        ]
        bit *= 2
    return values[0] + jnp.zeros(classes.shape, jnp.float32)


def velocity_of(spin, field):
    s0, s1, s2 = spin
    h0, h1, h2 = field
    t0 = s1 * h2 - s2 * h1
    t1 = s2 * h0 - s0 * h2
    t2 = s0 * h1 - s1 * h0
    return (
        -t0 - damping * (s1 * t2 - s2 * t1),
        -t1 - damping * (s2 * t0 - s0 * t2),
        -t2 - damping * (s0 * t1 - s1 * t0),
    )


def evolve_kernel(sizes, polar_in, azimuth_in, classes_in, table_ref, mid_ref, end_ref,
                  polar_ref, azimuth_ref, classes_ref, S, Q, J, GS, GQ, GJ, OS, OQ, ins, low, high, lowk, highk,
                  pack, left_pack, right_pack,
                  xs, xr, ys, yr, zs, zr, gs, gr, osem, isem):
    nx, ny, nz = sizes
    depth, wide, lanes = polar_ref.shape
    ext = wide + 2 * HALO
    tiles = ext // 8
    inner = wide // 8
    group = 2 * HALO
    me_x, me_y, me_z = lax.axis_index("gx"), lax.axis_index("gy"), lax.axis_index("gz")

    def at(axis, me, n, step):
        return {axis: lax.rem(me + (step + n), n)}

    x_left, x_right = at("gx", me_x, nx, -1), at("gx", me_x, nx, 1)
    y_left, y_right = at("gy", me_y, ny, -1), at("gy", me_y, ny, 1)
    z_down, z_up = at("gz", me_z, nz, -1), at("gz", me_z, nz, 1)

    fetches = [
        pltpu.make_async_copy(polar_in, polar_ref, isem.at[0]),
        pltpu.make_async_copy(azimuth_in, azimuth_ref, isem.at[1]),
        pltpu.make_async_copy(classes_in, classes_ref, isem.at[2]),
    ]
    for copy in fetches:
        copy.start()
    barrier = pltpu.get_barrier_semaphore()
    for who in (x_left, x_right, y_left, y_right, z_down, z_up):
        pl.semaphore_signal(barrier, inc=1, device_id=who, device_id_type=MESH)
    pl.semaphore_wait(barrier, 6)

    def remote(src, dst, send, recv, who):
        return pltpu.make_async_remote_copy(
            src_ref=src, dst_ref=dst, send_sem=send, recv_sem=recv, device_id=who, device_id_type=MESH
        )

    top = pl.ds(wide - HALO, HALO)
    bottom = pl.ds(0, HALO)
    x_copies = [
        remote(polar_in.at[:, top, :], low.at[0], xs.at[0], xr.at[0], x_right),
        remote(azimuth_in.at[:, top, :], low.at[1], xs.at[1], xr.at[1], x_right),
        remote(classes_in.at[pl.ds(0, 3), :, top, :], lowk.at[pl.ds(0, 3)], xs.at[2], xr.at[2], x_right),
        remote(classes_in.at[4, :, top, :], lowk.at[4], xs.at[6], xr.at[6], x_right),
        remote(classes_in.at[5, 0, top, :], lowk.at[5, 0], xs.at[7], xr.at[7], x_right),
        remote(polar_in.at[:, bottom, :], high.at[0], xs.at[3], xr.at[3], x_left),
        remote(azimuth_in.at[:, bottom, :], high.at[1], xs.at[4], xr.at[4], x_left),
        remote(classes_in.at[pl.ds(0, 3), :, bottom, :], highk.at[pl.ds(0, 3)], xs.at[5], xr.at[5], x_left),
        remote(classes_in.at[4, :, bottom, :], highk.at[4], xs.at[8], xr.at[8], x_left),
        remote(classes_in.at[5, 0, bottom, :], highk.at[5, 0], xs.at[9], xr.at[9], x_left),
    ]
    for copy in x_copies:
        copy.start()

    lane = lax.broadcasted_iota(jnp.int32, (8, lanes), 1)
    group_of = lane // group
    place = lane % group

    def spread(z, polar, azimuth, coupling_at, row):
        where_to = pl.ds(row, 8)
        shift = group * z + HALO
        mine = group_of == z
        spin = spins_of(polar, azimuth)
        for c in range(3):
            S[c, z + 1, where_to, :] = spin[c]
            old = pack[c, where_to, :]
            pack[c, where_to, :] = jnp.where(mine, pltpu.roll(spin[c], shift, 1), old)
        for d in range(6):
            value = coupling_at(d)
            J[d, z, where_to, :] = value
            old = pack[3 + d, where_to, :]
            pack[3 + d, where_to, :] = jnp.where(mine, pltpu.roll(value, shift, 1), old)

    pack[...] = jnp.zeros(pack.shape, jnp.float32)

    def own(z, carry):
        for r in range(inner):
            rows = pl.ds(8 * r, 8)
            spread(z, polar_ref[z, rows, :], azimuth_ref[z, rows, :],
                   lambda d: lookup(classes_ref[d, z, rows, :], table_ref), HALO + 8 * r)
        return carry

    for copy in fetches:
        copy.wait()
    lax.fori_loop(0, depth, own, 0)

    def y_copies(part):
        rows = (pl.ds(HALO, wide), pl.ds(0, HALO), pl.ds(HALO + wide, HALO))[part]
        made = [remote(pack.at[:, rows, :], left_pack.at[:, rows, :], ys.at[part], yr.at[part], y_right)]
        if ny > 2:
            made.append(remote(pack.at[:, rows, :], right_pack.at[:, rows, :], ys.at[3 + part], yr.at[3 + part], y_left))
        return made

    def z_copies(field, base):
        return [
            remote(field.at[:, 1], field.at[:, depth + 1], zs.at[base], zr.at[base], z_down),
            remote(field.at[:, depth], field.at[:, 0], zs.at[base + 1], zr.at[base + 1], z_up),
        ]

    def g_copy(ghost, other, base):
        return remote(ghost, other, gs.at[base], gr.at[base], z_up)

    for copy in y_copies(0):
        copy.start()
    for copy in x_copies:
        copy.wait()

    def edges(z, carry):
        def coupling_at(halo, row, d):
            if d == 3 and row > 0:
                return J[0, z, pl.ds(row - 1, 8), :]
            if d == 3:
                return pltpu.roll(J[0, z, pl.ds(row, 8), :], 1, 0)
            if d == 5:
                below = J[2, jnp.maximum(z - 1, 0), pl.ds(row, 8), :]
                return jnp.where(z == 0, lookup(halo[5, 0], table_ref), below)
            return lookup(halo[d, z], table_ref)

        spread(z, low[0, z], low[1, z], lambda d: coupling_at(lowk, 0, d), 0)
        spread(z, high[0, z], high[1, z], lambda d: coupling_at(highk, HALO + wide, d), HALO + wide)
        return carry

    lax.fori_loop(0, depth, edges, 0)
    for part in (1, 2):
        for copy in y_copies(part):
            copy.start()
    for copy in z_copies(S, 0):
        copy.start()
    for part in range(3):
        for copy in y_copies(part):
            copy.wait()
    from_right = left_pack if ny == 2 else right_pack

    def ghosts(r, carry):
        rows = pl.ds(pl.multiple_of(8 * r, 8), 8)
        for f in range(9):
            value = jnp.where(place < HALO, left_pack[f, rows, :], from_right[f, rows, :])
            if f < 3:
                GS[f, rows, :] = value
            else:
                GJ[f - 3, rows, :] = value
        return carry

    lax.fori_loop(0, tiles, ghosts, 0)
    g_copy(GS, OS, 0).start()

    def x_pair(ref, r, value):
        if r < tiles - 1:
            ahead = ref[pl.ds(8 * r + 1, 8), :]
        else:
            ahead = pltpu.roll(value, 7, 0)
        if r > 0:
            behind = ref[pl.ds(8 * r - 1, 8), :]
        else:
            behind = pltpu.roll(value, 1, 0)
        return ahead, behind

    def plane(F, G, z, finish):
        up_shift = lanes - (group * z + HALO)
        left_mask = lane == group * z + HALO - 1
        right_mask = lane == group * z + HALO
        for r in range(tiles):
            rows = pl.ds(8 * r, 8)
            coupling = [J[d, z, rows, :] for d in range(6)]
            spin, field = [], []
            for c in range(3):
                M = F[c, z + 1, rows, :]
                ahead, behind = x_pair(F.at[c, z + 1], r, M)
                U = pltpu.roll(G[c, rows, :], up_shift, 1)
                right = pltpu.roll(jnp.where(lane == 0, U, M), lanes - 1, 1)
                left = pltpu.roll(jnp.where(lane == lanes - 1, U, M), 1, 1)
                total = coupling[0] * ahead + coupling[1] * right
                total = total + coupling[2] * F[c, z + 2, rows, :]
                total = total + coupling[3] * behind
                total = total + coupling[4] * left
                total = total + coupling[5] * F[c, z, rows, :]
                ins[c, rows, :] = jnp.where(
                    left_mask, pltpu.roll(M, group * z + HALO - 1, 1),
                    jnp.where(right_mask, pltpu.roll(M, group * z + HALO + 1, 1), ins[c, rows, :]))
                spin.append(M)
                field.append(total)
            finish(spin, velocity_of(spin, field), z, rows)

    def ghost_pass(G, other, finish):
        for r in range(tiles):
            rows = pl.ds(8 * r, 8)
            coupling = [GJ[d, rows, :] for d in range(6)]
            spin, field = [], []
            for c in range(3):
                M = G[c, rows, :]
                O = other[c, rows, :]
                I = ins[c, rows, :]
                ahead, behind = x_pair(G.at[c], r, M)
                right = jnp.where(place == HALO - 1, I, pltpu.roll(M, lanes - 1, 1))
                left = jnp.where(place == HALO, I, pltpu.roll(M, 1, 1))
                above = pltpu.roll(jnp.where(lane >= group, M, O), lanes - group, 1)
                below = pltpu.roll(jnp.where(lane < lanes - group, M, O), group, 1)
                total = coupling[0] * ahead + coupling[1] * right
                total = total + coupling[2] * above
                total = total + coupling[3] * behind
                total = total + coupling[4] * left
                total = total + coupling[5] * below
                spin.append(M)
                field.append(total)
            finish(spin, velocity_of(spin, field), rows)

    def predict(spin, speed, z, rows):
        for c in range(3):
            Q[c, z + 1, rows, :] = spin[c] + time_step * speed[c]

    def predict_ghost(spin, speed, rows):
        for c in range(3):
            GQ[c, rows, :] = spin[c] + time_step * speed[c]

    def correct(spin, speed, z, rows):
        for c in range(3):
            S[c, z + 1, rows, :] = 0.5 * (S[c, z + 1, rows, :] + spin[c]) + 0.5 * time_step * speed[c]

    def correct_ghost(spin, speed, rows):
        for c in range(3):
            GS[c, rows, :] = 0.5 * (GS[c, rows, :] + spin[c]) + 0.5 * time_step * speed[c]

    ins[...] = jnp.zeros(ins.shape, jnp.float32)

    def stage(F, G, O, base, finish, finish_ghost, send_main, send_ghost):
        def inside(z, carry):
            plane(F, G, z, finish)
            return carry

        def outside(i, carry):
            plane(F, G, i * (depth - 1), finish)
            return carry

        lax.fori_loop(1, depth - 1, inside, 0)
        for copy in z_copies(F, 2 * base):
            copy.wait()
        lax.fori_loop(0, 2, outside, 0)
        send_main()
        g_copy(G, O, base).wait()
        ghost_pass(G, O, finish_ghost)
        send_ghost()

    def out_copy(target):
        return pltpu.make_async_copy(S.at[:, pl.ds(1, depth), pl.ds(HALO, wide), :], target, osem.at[0])

    def step(turn, carry):
        def send_q():
            for copy in z_copies(Q, 2):
                copy.start()

        def send_s():
            @pl.when(turn < STEPS - 1)
            def _():
                for copy in z_copies(S, 0):
                    copy.start()

        def send_gs():
            @pl.when(turn < STEPS - 1)
            def _():
                g_copy(GS, OS, 0).start()

        stage(S, GS, OS, 0, predict, predict_ghost, send_q, lambda: g_copy(GQ, OQ, 1).start())

        @pl.when(turn == 2)
        def _():
            out_copy(mid_ref).wait()

        stage(Q, GQ, OQ, 1, correct, correct_ghost, send_s, send_gs)

        @pl.when(turn == 1)
        def _():
            out_copy(mid_ref).start()

        return carry

    lax.fori_loop(0, STEPS, step, 0)
    out_copy(end_ref).start()
    out_copy(end_ref).wait()


def evolve(polar_angle, azimuth, classes, exchange_table):
    depth, wide, lanes = polar_angle.shape
    sizes = (lax.axis_size("gx"), lax.axis_size("gy"), lax.axis_size("gz"))
    assert sizes[2] == 2 and depth * 2 * HALO == lanes
    ext = wide + 2 * HALO
    f32 = jnp.float32
    out = jax.ShapeDtypeStruct((3, depth, wide, lanes), f32)
    hbm = pl.BlockSpec(memory_space=pltpu.HBM)
    anywhere = pl.BlockSpec(memory_space=pl.ANY)
    V = pltpu.VMEM
    D = pltpu.SemaphoreType.DMA
    return pl.pallas_call(
        functools.partial(evolve_kernel, sizes),
        out_shape=(out, out),
        in_specs=[hbm, hbm, hbm, pl.BlockSpec(memory_space=pltpu.SMEM)],
        out_specs=(anywhere, anywhere),
        scratch_shapes=[
            V((depth, wide, lanes), f32), V((depth, wide, lanes), f32), V((6, depth, wide, lanes), jnp.int32),
            V((3, depth + 2, ext, lanes), f32), V((3, depth + 2, ext, lanes), f32),
            V((6, depth, ext, lanes), f32),
            V((3, ext, lanes), f32), V((3, ext, lanes), f32), V((6, ext, lanes), f32),
            V((3, ext, lanes), f32), V((3, ext, lanes), f32), V((3, ext, lanes), f32),
            V((2, depth, HALO, lanes), f32), V((2, depth, HALO, lanes), f32),
            V((6, depth, HALO, lanes), jnp.int32), V((6, depth, HALO, lanes), jnp.int32),
            V((9, ext, lanes), f32), V((9, ext, lanes), f32), V((9, ext, lanes), f32),
            D((10,)), D((10,)), D((6,)), D((6,)), D((4,)), D((4,)), D((2,)), D((2,)), D((1,)), D((3,)),
        ],
        compiler_params=pltpu.CompilerParams(collective_id=0, has_side_effects=True, vmem_limit_bytes=65200000),
        name="evolve",
    )(polar_angle, azimuth, classes, exchange_table)


def phase_table(wave_count, total_length):
    index = np.arange(total_length)[:, None] * np.arange(wave_count)[None, :] % total_length
    phase = index * (2.0 * math.pi / total_length)
    return np.cos(phase).astype(np.float32), np.sin(phase).astype(np.float32)


def exact_dot(a, b):
    return jnp.dot(a, b, precision=lax.Precision.HIGHEST, preferred_element_type=jnp.float32)


def modes_kernel(sizes, scale, mid_ref, end_ref, x_in, y_in, cos_ref, sin_ref, out_ref,
                 x_ref, y_ref, T, R, Z, D, DR, E, F, zs, zr, xs, xr, ys, yr, fs, fr, isem):
    nx, ny, nz = sizes
    depth, wide, lanes = mid_ref.shape[1:]
    owned = D.shape[2]
    half = KX // nz
    me_x, me_y, me_z = lax.axis_index("gx"), lax.axis_index("gy"), lax.axis_index("gz")
    peers_x = [{"gx": lax.rem(me_x + o, nx)} for o in range(1, nx)]
    peers_y = [{"gy": lax.rem(me_y + o, ny)} for o in range(1, ny)]
    twin = {"gz": 1 - me_z}
    fetches = [
        pltpu.make_async_copy(x_in.at[me_x], x_ref, isem.at[0]),
        pltpu.make_async_copy(y_in.at[me_y], y_ref, isem.at[1]),
    ]
    for copy in fetches:
        copy.start()

    barrier = pltpu.get_barrier_semaphore()
    for who in peers_x + peers_y + [twin]:
        pl.semaphore_signal(barrier, inc=1, device_id=who, device_id_type=MESH)
    pl.semaphore_wait(barrier, nx + ny - 1)

    def remote(src, dst, send, recv, who):
        return pltpu.make_async_remote_copy(
            src_ref=src, dst_ref=dst, send_sem=send, recv_sem=recv, device_id=who, device_id_type=MESH
        )

    lane = lax.broadcasted_iota(jnp.int32, (half, 4 * KY), 1)
    cosine_lane = (lane // KY) % 2 == 0
    for copy in fetches:
        copy.wait()
    table = x_ref[...]
    swaps, x_copies, y_copies, shares = [], [], [], []

    def transform(c):
        for z in range(depth):
            for turn, ref in enumerate((mid_ref, end_ref)):
                along_x = exact_dot(table, ref[c, z])
                T[pl.ds(z * KX, KX), pl.ds(2 * lanes * turn, lanes)] = along_x[:KX]
                T[pl.ds(z * KX, KX), pl.ds(2 * lanes * turn + lanes, lanes)] = along_x[KX:]
        parts = exact_dot(T[...], y_ref[...]).reshape(depth, nz, half, 4 * KY)
        for h in range(nz):
            R[h, c] = parts[:, h]
        swaps.append(remote(R.at[1 - me_z, c], Z.at[c], zs.at[c], zr.at[c], twin))
        swaps[c].start()

    def waves(c):
        swaps[c].wait()
        ones, twos = [], []
        for z in range(nz * depth):
            own = R[me_z, c, z] if z < depth else Z[c, z - depth]
            ones.append(own)
            twos.append(jnp.where(cosine_lane, -pltpu.roll(own, 3 * KY, 1), pltpu.roll(own, KY, 1)))

        def block_of(block, carry):
            for k in range(owned):
                total = None
                for z in range(nz * depth):
                    where_z = me_z * depth + z if z < depth else (1 - me_z) * depth + z - depth
                    wave = block * owned + k
                    term = cos_ref[wave, where_z] * ones[z] + sin_ref[wave, where_z] * twos[z]
                    total = term if total is None else total + term
                D[c, block, k] = total
            return carry

        lax.fori_loop(0, nx, block_of, 0)
        x_copies.append([
            remote(D.at[c, lax.rem(me_x + o, nx)], DR.at[c, o - 1], xs.at[c, o - 1], xr.at[c, o - 1], peers_x[o - 1])
            for o in range(1, nx)
        ])
        for copy in reversed(x_copies[c]):
            copy.start()

    def sum_x(c):
        for copy in x_copies[c]:
            copy.wait()
        total = D[c, me_x]
        for o in range(1, nx):
            total = total + DR[c, o - 1]
        E[c, me_y] = total
        y_copies.append([
            remote(E.at[c, me_y], E.at[c, me_y], ys.at[c, o - 1], yr.at[c, o - 1], peers_y[o - 1])
            for o in range(1, ny)
        ])
        for copy in y_copies[c]:
            copy.start()

    def sum_y(c):
        for copy in y_copies[c]:
            copy.wait()
        total = E[c, 0]
        for o in range(1, ny):
            total = total + E[c, o]
        F[c, me_z] = total * jnp.where(cosine_lane, scale, -scale)
        shares.append(remote(F.at[c, me_z], F.at[c, me_z], fs.at[c], fr.at[c], twin))
        shares[c].start()

    transform(0)
    transform(1)
    waves(0)
    transform(2)
    waves(1)
    waves(2)
    sum_x(0)
    sum_x(1)
    sum_y(0)
    sum_x(2)
    sum_y(1)
    sum_y(2)
    for c in range(3):
        shares[c].wait()
        out_ref[:, :, c] = F[c]


def modes(spin_mid, spin_end):
    depth, wide, lanes = spin_mid.shape[1:]
    sizes = nx, ny, nz = (lax.axis_size("gx"), lax.axis_size("gy"), lax.axis_size("gz"))
    total_z = depth * nz
    owned = total_z // nx
    half = KX // nz
    f32 = jnp.float32
    x_cos, x_sin = phase_table(KX, wide * nx)
    y_cos, y_sin = phase_table(KY, lanes * ny)
    z_cos, z_sin = phase_table(total_z, total_z)
    x_full = np.concatenate([x_cos, x_sin], 1).reshape(nx, wide, 2 * KX).transpose(0, 2, 1)
    y_pair = np.stack([
        np.concatenate([y_cos, y_sin], 1).reshape(ny, lanes, 2 * KY),
        np.concatenate([-y_sin, y_cos], 1).reshape(ny, lanes, 2 * KY),
    ], 1).reshape(ny, 2 * lanes, 2 * KY)
    y_full = np.zeros((ny, 4 * lanes, 4 * KY), np.float32)
    y_full[:, : 2 * lanes, : 2 * KY] = y_pair
    y_full[:, 2 * lanes :, 2 * KY :] = y_pair
    scale = float(wide * nx * lanes * ny * total_z) ** -0.5
    vmem = pl.BlockSpec(memory_space=pltpu.VMEM)
    smem = pl.BlockSpec(memory_space=pltpu.SMEM)
    hbm = pl.BlockSpec(memory_space=pltpu.HBM)
    V, DMA = pltpu.VMEM, pltpu.SemaphoreType.DMA
    width = 4 * KY
    out = pl.pallas_call(
        functools.partial(modes_kernel, sizes, scale),
        out_shape=jax.ShapeDtypeStruct((nz, owned, 3, half, width), f32),
        in_specs=[vmem, vmem, hbm, hbm, smem, smem],
        out_specs=vmem,
        scratch_shapes=[
            V((2 * KX, wide), f32), V((4 * lanes, width), f32),
            V((depth * KX, 4 * lanes), f32), V((nz, 3, depth, half, width), f32),
            V((3, depth, half, width), f32), V((3, nx, owned, half, width), f32),
            V((3, nx - 1, owned, half, width), f32), V((3, ny, owned, half, width), f32),
            V((3, nz, owned, half, width), f32),
            DMA((3,)), DMA((3,)), DMA((3, nx - 1)), DMA((3, nx - 1)), DMA((3, ny - 1)), DMA((3, ny - 1)),
            DMA((3,)), DMA((3,)), DMA((2,)),
        ],
        compiler_params=pltpu.CompilerParams(collective_id=1, has_side_effects=True, vmem_limit_bytes=32 * 1024 * 1024),
        name="modes",
    )(spin_mid, spin_end, jnp.asarray(x_full), jnp.asarray(y_full), jnp.asarray(z_cos.T), jnp.asarray(z_sin.T))
    out = out.reshape(nz, owned, 3, half, 2, 2, KY).transpose(4, 1, 5, 2, 0, 3, 6)
    return out.reshape(2, owned, -1)


def body(polar_angle, azimuth, classes, exchange_table):
    spin_mid, spin_end = evolve(polar_angle, azimuth, classes, exchange_table)
    both = modes(spin_mid, spin_end)
    return (spin_end, both[0], both[1])


def solution(mesh):
    return jax.shard_map(
        body,
        mesh=mesh,
        in_specs=(
            P("gz", ("groups", "gx"), "gy"),
            P("gz", ("groups", "gx"), "gy"),
            P(None, "gz", ("groups", "gx"), "gy"),
            P(),
        ),
        out_specs=(
            P(None, "gz", ("groups", "gx"), "gy"),
            P(("groups", "gx"), None),
            P(("groups", "gx"), None),
        ),
        check_vma=False,
    )
```

profile of v0, /device:TPU:0, one launch (start us, length us, event | category | flops | bytes accessed | tf_op | source)
XLA Modules:
  0.0 72.0 jit_solution(222464935238934042)
XLA Ops:
  0.6 0.0 copy-start.5
  0.6 0.0 copy-start.6
  0.7 0.0 copy-start.3
  0.7 0.0 copy-start.4
  0.7 43.1 %evolve.1 = (f32[3,8,64,128]{3,2,1,0:T(8,128)}, f32[3,8,64,128]{3,2,1,0:T(8,128)}) custom-call(f32[8,64,128]{2,1,0:T(8,128)} %polar_in.1, f32[8,64,128]{2,1,0:T(8,128)} %azimuth_in.1, s32[6,8,64,128]{3,2,1,0:T(8,128)} %classes_in.1, f32[8]{0:T(128)} %table_ref.1), custom_call_target="tpu_custom_call" | custom-call | tf_op jit(solution)/shard_map/evolve/pallas_call | solution.py:365
  43.8 0.0 copy-done.5
  43.8 0.0 copy-done.6
  43.8 0.0 copy-done.3
  43.8 0.0 copy-done.4
  43.8 0.0 copy-start
  43.8 1.1 %copy-done = f32[3,8,64,128]{3,2,1,0:T(8,128)S(1)} copy-done((f32[3,8,64,128]{3,2,1,0:T(8,128)S(1)}, f32[3,8,64,128]{3,2,1,0:T(8,128)}, u32[]{:S(2)}) %copy-start) | copy-done | bytes 786456
  45.0 0.0 copy-start.2
  45.0 1.1 %copy-done.2 = f32[3,8,64,128]{3,2,1,0:T(8,128)S(1)} copy-done((f32[3,8,64,128]{3,2,1,0:T(8,128)S(1)}, f32[3,8,64,128]{3,2,1,0:T(8,128)}, u32[]{:S(2)}) %copy-start.2) | copy-done | bytes 786456
  46.1 22.1 %modes.1 = f32[2,4,3,16,128]{4,3,2,1,0:T(8,128)S(1)} custom-call(f32[3,8,64,128]{3,2,1,0:T(8,128)S(1)} %copy-done.2, f32[3,8,64,128]{3,2,1,0:T(8,128)S(1)} %copy-done, f32[4,64,64]{2,1,0:T(8,128)S(1)} %copy-done.4, f32[2,512,128]{2,1,0:T(8,128)S(1)} %copy-done.3, f32[16,16]{1,0:T(8,128)S(1)} %copy-done.6, f32[16,16]{1,0:T(8,128)S(1)} %copy-done.5), custom_call_target="tpu_custom_call" | custom-call | tf_op jit(solution)/shard_map/modes/pallas_call | solution.py:534
  68.2 0.6 reshape.14
  68.9 0.4 fusion
  69.3 0.0 copy-start.1
  69.4 0.9 %squeeze.7 = f32[4,6144]{1,0:T(4,128)} reshape(f32[1,4,2,3,2,16,32]{6,5,4,3,2,1,0:T(8,128)S(1)} %copy.12) | data formatting | bytes 196608 | tf_op jit(solution)/shard_map/squeeze | solution.py:558
  70.2 0.9 %squeeze.6 = f32[4,6144]{1,0:T(4,128)} reshape(f32[1,4,2,3,2,16,32]{6,5,4,3,2,1,0:T(8,128)S(1)} %copy.11) | data formatting | bytes 196608 | tf_op jit(solution)/shard_map/squeeze | solution.py:558
  71.1 0.0 copy-done.1
  71.1 0.9 %copy.14 = f32[3,8,64,128]{3,2,1,0:T(8,128)} copy(f32[3,8,64,128]{3,2,1,0:T(8,128)S(1)} %copy-done.1) | data formatting | bytes 1572864
  (2 shorter events, 0.1 us)
Async XLA Ops:
  0.6 43.2 %copy-start.5 = (f32[16,16]{1,0:T(8,128)S(1)}, f32[16,16]{1,0:T(8,128)}, u32[]{:S(2)}) copy-start(f32[16,16]{1,0:T(8,128)} %constant.11.clone.sin_ref) | copy-start | bytes 3076
  0.6 43.2 %copy-start.6 = (f32[16,16]{1,0:T(8,128)S(1)}, f32[16,16]{1,0:T(8,128)}, u32[]{:S(2)}) copy-start(f32[16,16]{1,0:T(8,128)} %constant.10.clone.cos_ref) | copy-start | bytes 3076
  0.7 43.2 %copy-start.3 = (f32[2,512,128]{2,1,0:T(8,128)S(1)}, f32[2,512,128]{2,1,0:T(8,128)}, u32[]{:S(2)}) copy-start(f32[2,512,128]{2,1,0:T(8,128)} %constant.9.clone.y_in) | copy-start | bytes 1572868
  0.7 43.2 %copy-start.4 = (f32[4,64,64]{2,1,0:T(8,128)S(1)}, f32[4,64,64]{2,1,0:T(8,128)}, u32[]{:S(2)}) copy-start(f32[4,64,64]{2,1,0:T(8,128)} %constant.8.clone.x_in) | copy-start | bytes 196612
  43.8 1.1 %copy-start = (f32[3,8,64,128]{3,2,1,0:T(8,128)S(1)}, f32[3,8,64,128]{3,2,1,0:T(8,128)}, u32[]{:S(2)}) copy-start(f32[3,8,64,128]{3,2,1,0:T(8,128)} %get-tuple-element.12.end_ref) | copy-start | bytes 2359300
  45.0 1.1 %copy-start.2 = (f32[3,8,64,128]{3,2,1,0:T(8,128)S(1)}, f32[3,8,64,128]{3,2,1,0:T(8,128)}, u32[]{:S(2)}) copy-start(f32[3,8,64,128]{3,2,1,0:T(8,128)} %get-tuple-element.6.mid_ref) | copy-start | bytes 2359300
  69.3 1.8 %copy-start.1 = (f32[3,8,64,128]{3,2,1,0:T(8,128)S(1)}, f32[3,8,64,128]{3,2,1,0:T(8,128)}, u32[]{:S(2)}) copy-start(f32[3,8,64,128]{3,2,1,0:T(8,128)} %get-tuple-element.12.end_ref) | copy-start | bytes 2359300
where the time goes:
time: 72.2 us; the launch traced here: 72 us
  Pallas kernels  65.2 us (90%)
  local copies, waits for them, and re-layouts  6 us (8%)
  between operations  0.76 us (1%)
    pallas_call x1, Pallas kernels, evolve(): pl.pallas_call(functools.partial(evolve_kernel, sizes), out_shape=(out, o...  43.1 us
    pallas_call x1, Pallas kernels, modes(): pl.pallas_call(functools.partial(modes_kernel, sizes, scale), out_shape=j...  22.1 us
    unnamed x15, local copies, waits for them, and re-layouts  3.17 us
    squeeze x2, local copies, waits for them, and re-layouts, body(): return (spin_end, both[0], both[1])  1.7 us

commit v1 on v0

v1 whole, which is shorter than its diff:
```python
import functools
import math

import jax
import jax.numpy as jnp
import numpy as np
from jax import lax
from jax.experimental import pallas as pl
from jax.experimental.pallas import tpu as pltpu
from jax.sharding import PartitionSpec as P

KX = 32
KY = 32
STEPS = 4
HALO = 8
MESH = pl.DeviceIdType.MESH

time_step = 0.1
damping = 0.1
HALF_SINE = (0.4999999978578703, -0.02083332246217966, 0.00026040783166918343, -1.5475817235376e-06,
             5.0882140435283864e-09)
HALF_COSINE = (0.9999999997798975, -0.12499999839235146, 0.0026041647630212603, -2.1700563804658615e-05,
               9.671927783275375e-08, -2.5440497387766775e-10)


def horner(coefficients, square):
    total = coefficients[-1]
    for value in coefficients[-2::-1]:
        total = total * square + value
    return total


def sin_cos(angle):
    square = angle * angle
    half_sine = angle * horner(HALF_SINE, square)
    half_cosine = horner(HALF_COSINE, square)
    twice = half_sine + half_sine
    return twice * half_cosine, 1.0 - twice * half_sine


def spins_of(polar, azimuth):
    sine_polar, cosine_polar = sin_cos(polar)
    sine_azimuth, cosine_azimuth = sin_cos(azimuth)
    scaled = sine_polar * damping
    return scaled * cosine_azimuth, scaled * sine_azimuth, cosine_polar * damping


def descent(spin, field):
    s0, s1, s2 = spin
    h0, h1, h2 = field
    w0 = h0 + (s1 * h2 - s2 * h1)
    w1 = h1 + (s2 * h0 - s0 * h2)
    w2 = h2 + (s0 * h1 - s1 * h0)
    return s1 * w2 - s2 * w1, s2 * w0 - s0 * w2, s0 * w1 - s1 * w0


def evolve_kernel(sizes, polar_in, azimuth_in, classes_in, table_ref, mid_ref, end_ref,
                  polar_ref, azimuth_ref, classes_ref, S, Q, J, GS, GQ, GJ, OS, OQ, OJ,
                  low, high, lowk, highk, pack, left_pack, right_pack, out,
                  xs, xr, ys, yr, zs, zr, gs, gr, osem, isem):
    nx, ny, nz = sizes
    depth, wide, lanes = polar_ref.shape
    ext = wide + 2 * HALO
    tiles = ext // 8
    inner = wide // 8
    group = 2 * HALO
    me_x, me_y, me_z = lax.axis_index("gx"), lax.axis_index("gy"), lax.axis_index("gz")

    def at(axis, me, n, step):
        return {axis: lax.rem(me + (step + n), n)}

    x_left, x_right = at("gx", me_x, nx, -1), at("gx", me_x, nx, 1)
    y_left, y_right = at("gy", me_y, ny, -1), at("gy", me_y, ny, 1)
    z_down, z_up = at("gz", me_z, nz, -1), at("gz", me_z, nz, 1)
    sides = [y_right] if ny == 2 else [y_right, y_left]

    fetches = [
        pltpu.make_async_copy(polar_in, polar_ref, isem.at[0]),
        pltpu.make_async_copy(azimuth_in, azimuth_ref, isem.at[1]),
        pltpu.make_async_copy(classes_in.at[pl.ds(0, 3)], classes_ref.at[pl.ds(0, 3)], isem.at[2]),
        pltpu.make_async_copy(classes_in.at[4], classes_ref.at[3], isem.at[3]),
        pltpu.make_async_copy(classes_in.at[5, 0], classes_ref.at[4, 0], isem.at[4]),
    ]
    for copy in fetches:
        copy.start()
    barrier = pltpu.get_barrier_semaphore()
    friends = [x_left, x_right, z_up] + sides + [{**x, **y} for x in (x_left, x_right) for y in sides]
    for who in friends:
        pl.semaphore_signal(barrier, inc=1, device_id=who, device_id_type=MESH)
    pl.semaphore_wait(barrier, len(friends))

    def remote(src, dst, send, recv, who):
        return pltpu.make_async_remote_copy(
            src_ref=src, dst_ref=dst, send_sem=send, recv_sem=recv, device_id=who, device_id_type=MESH
        )

    top = pl.ds(wide - HALO, HALO)
    bottom = pl.ds(0, HALO)
    x_copies = []
    for rows, halo, kinds, who in ((top, low, lowk, x_right), (bottom, high, highk, x_left)):
        for src, dst in (
            (polar_in.at[:, rows, :], halo.at[0]),
            (azimuth_in.at[:, rows, :], halo.at[1]),
            (classes_in.at[pl.ds(0, 3), :, rows, :], kinds.at[pl.ds(0, 3)]),
            (classes_in.at[5, 0, rows, :], kinds.at[3, 0]),
        ):
            i = len(x_copies)
            x_copies.append(remote(src, dst, xs.at[i], xr.at[i], who))
    for copy in x_copies:
        copy.start()

    lane = lax.broadcasted_iota(jnp.int32, (8, lanes), 1)
    group_of = lane // group
    place = lane % group
    ratio = time_step / damping
    table = jnp.zeros((8, lanes), jnp.float32)
    for i in range(table_ref.shape[0]):
        table = jnp.where(lane == i, table_ref[i] * ratio, table)

    def lookup(kinds):
        return jnp.take_along_axis(table, kinds, axis=1, mode="promise_in_bounds")

    for f in range(5):
        for r in range(inner):
            pack[f, pl.ds(8 * r, 8), :] = jnp.zeros((8, lanes), jnp.float32)
    for copy in fetches:
        copy.wait()

    def own_first(z, carry):
        mine = group_of == z
        mirror = (group * z + HALO - 1 + lanes - lane) % lanes
        for r in range(inner):
            rows = pl.ds(8 * r, 8)
            values = [polar_ref[z, rows, :], azimuth_ref[z, rows, :]]
            for d in range(3):
                value = lookup(classes_ref[d, z, rows, :])
                J[d, z + 1, pl.ds(HALO + 8 * r, 8), :] = value
                values.append(value)
            for f, value in enumerate(values):
                turned = jnp.take_along_axis(value, mirror, axis=1, mode="promise_in_bounds")
                pack[f, rows, :] = jnp.where(mine, turned, pack[f, rows, :])
        return carry

    lax.fori_loop(0, depth, own_first, 0)

    y_copies = []
    for side, (who, target) in enumerate(zip(sides, (left_pack, right_pack))):
        for part, (src, dst, to) in enumerate((
            (top, pl.ds(0, HALO), {**x_right, **who}),
            (bottom, pl.ds(HALO + wide, HALO), {**x_left, **who}),
            (pl.ds(0, wide), pl.ds(HALO, wide), who),
        )):
            i = 3 * side + part
            y_copies.append(remote(pack.at[:, src, :], target.at[:, dst, :], ys.at[i], yr.at[i], to))
    for copy in y_copies:
        copy.start()

    def own_second(z, carry):
        for r in range(inner):
            rows = pl.ds(8 * r, 8)
            spin = spins_of(polar_ref[z, rows, :], azimuth_ref[z, rows, :])
            for c in range(3):
                S[c, z + 1, pl.ds(HALO + 8 * r, 8), :] = spin[c]
            J[3, z + 1, pl.ds(HALO + 8 * r, 8), :] = lookup(classes_ref[3, z, rows, :])
        return carry

    lax.fori_loop(0, depth, own_second, 0)
    for r in range(inner):
        J[2, 0, pl.ds(HALO + 8 * r, 8), :] = lookup(classes_ref[4, 0, pl.ds(8 * r, 8), :])
    for copy in x_copies:
        copy.wait()

    def edges(z, carry):
        for halo, kinds, row in ((low, lowk, 0), (high, highk, HALO + wide)):
            spin = spins_of(halo[0, z], halo[1, z])
            for c in range(3):
                S[c, z + 1, pl.ds(row, 8), :] = spin[c]
            for d in range(3):
                J[d, z + 1, pl.ds(row, 8), :] = lookup(kinds[d, z])
        return carry

    lax.fori_loop(0, depth, edges, 0)
    J[2, 0, pl.ds(0, 8), :] = lookup(lowk[3, 0])
    J[2, 0, pl.ds(HALO + wide, 8), :] = lookup(highk[3, 0])

    def z_copies(field, base):
        return [
            remote(field.at[:, 1], field.at[:, depth + 1], zs.at[base], zr.at[base], z_down),
            remote(field.at[:, depth], field.at[:, 0], zs.at[base + 1], zr.at[base + 1], z_up),
        ]

    def g_copy(ghost, other, base):
        return remote(ghost, other, gs.at[base], gr.at[base], z_up)

    for copy in z_copies(S, 0):
        copy.start()
    for copy in y_copies:
        copy.wait()
    from_right = left_pack if ny == 2 else right_pack

    def ghosts(r, carry):
        rows = pl.ds(pl.multiple_of(8 * r, 8), 8)
        fields = [jnp.where(place >= HALO, left_pack[f, rows, :], from_right[f, rows, :]) for f in range(5)]
        spin = spins_of(fields[0], fields[1])
        for c in range(3):
            GS[c, rows, :] = spin[c]
        for d in range(3):
            GJ[d, rows, :] = fields[2 + d]
        edge = jnp.zeros((8, lanes), jnp.float32)
        for z in range(depth):
            edge = jnp.where(group_of == z, pltpu.roll(J[1, z + 1, rows, :], group * z + HALO, 1), edge)
        GJ[3, rows, :] = jnp.where(place == HALO - 1, edge, pltpu.roll(fields[3], lanes - 1, 1))
        return carry

    lax.fori_loop(0, tiles, ghosts, 0)
    g_copy(GS, OS, 0).start()
    g_copy(GJ.at[2], OJ, 2).start()

    def corners(z, carry):
        for row in (0, HALO + wide):
            rows = pl.ds(row, 8)
            outside = pltpu.roll(GJ[1, rows, :], lanes - (group * z + HALO), 1)
            J[3, z + 1, rows, :] = jnp.where(lane == 0, outside, pltpu.roll(J[1, z + 1, rows, :], 1, 1))
        return carry

    lax.fori_loop(0, depth, corners, 0)

    def x_pair(ref, r, value):
        ahead = ref[pl.ds(8 * r + 1, 8), :] if r < tiles - 1 else pltpu.roll(value, 7, 0)
        behind = ref[pl.ds(8 * r - 1, 8), :] if r > 0 else pltpu.roll(value, 1, 0)
        return ahead, behind

    def plane(F, G, z, finish, rows_of):
        up_shift = lanes - (group * z + HALO)
        for r in rows_of:
            rows = pl.ds(8 * r, 8)
            c0, c1, c2, c4 = (J[d, z + 1, rows, :] for d in range(4))
            c3 = J[0, z + 1, pl.ds(8 * r - 1, 8), :] if r > 0 else pltpu.roll(c0, 1, 0)
            c5 = J[2, z, rows, :]
            spin, field = [], []
            for c in range(3):
                M = F[c, z + 1, rows, :]
                ahead, behind = x_pair(F.at[c, z + 1], r, M)
                U = pltpu.roll(G[c, rows, :], up_shift, 1)
                right = jnp.where(lane == lanes - 1, U, pltpu.roll(M, lanes - 1, 1))
                left = jnp.where(lane == 0, U, pltpu.roll(M, 1, 1))
                total = (c0 * ahead + c3 * behind) + (c2 * F[c, z + 2, rows, :] + c5 * F[c, z, rows, :])
                total = total + (c1 * right + c4 * left)
                spin.append(M)
                field.append(total)
            finish(spin, descent(spin, field), z, rows)

    def ghost_pass(F, G, other, finish):
        for r in range(tiles):
            rows = pl.ds(8 * r, 8)
            c0, c1, c2, c4 = (GJ[d, rows, :] for d in range(4))
            c3 = GJ[0, pl.ds(8 * r - 1, 8), :] if r > 0 else pltpu.roll(c0, 1, 0)
            c5 = pltpu.roll(jnp.where(lane < lanes - group, c2, OJ[rows, :]), group, 1)
            spin, field = [], []
            for c in range(3):
                M = G[c, rows, :]
                O = other[c, rows, :]
                I = M
                for z in range(depth):
                    I = jnp.where(group_of == z, pltpu.roll(F[c, z + 1, rows, :], group * z + HALO, 1), I)
                ahead, behind = x_pair(G.at[c], r, M)
                right = jnp.where(place == HALO, I, pltpu.roll(M, 1, 1))
                left = jnp.where(place == HALO - 1, I, pltpu.roll(M, lanes - 1, 1))
                above = pltpu.roll(jnp.where(lane >= group, M, O), lanes - group, 1)
                below = pltpu.roll(jnp.where(lane < lanes - group, M, O), group, 1)
                total = (c0 * ahead + c3 * behind) + (c2 * above + c5 * below)
                total = total + (c1 * right + c4 * left)
                spin.append(M)
                field.append(total)
            finish(spin, descent(spin, field), rows)

    def predict(spin, change, z, rows):
        for c in range(3):
            Q[c, z + 1, rows, :] = spin[c] - change[c]

    def predict_ghost(spin, change, rows):
        for c in range(3):
            GQ[c, rows, :] = spin[c] - change[c]

    def correct(spin, change, z, rows):
        for c in range(3):
            S[c, z + 1, rows, :] = 0.5 * (S[c, z + 1, rows, :] + (spin[c] - change[c]))

    def correct_ghost(spin, change, rows):
        for c in range(3):
            GS[c, rows, :] = 0.5 * (GS[c, rows, :] + (spin[c] - change[c]))

    def stage(F, G, O, base, finish, finish_ghost, send_main, send_ghost, first=None):
        every = range(tiles)

        def inside(i, carry):
            plane(F, G, 2 * i + 1, finish, every)
            plane(F, G, 2 * i + 2, finish, every)
            return carry

        lax.fori_loop(0, (depth - 2) // 2, inside, 0)
        for copy in z_copies(F, 2 * base):
            copy.wait()
        plane(F, G, 0, finish, every)
        plane(F, G, depth - 1, finish, every)
        send_main()
        g_copy(G, O, base).wait()
        if first is not None:
            first()
        ghost_pass(F, G, O, finish_ghost)
        send_ghost()

    def publish(target, sem):
        copy = pltpu.make_async_copy(out, target, sem)

        def scaled(z, carry):
            for c in range(3):
                for r in range(inner):
                    out[c, z, pl.ds(8 * r, 8), :] = S[c, z + 1, pl.ds(HALO + 8 * r, 8), :] * (1.0 / damping)
            return carry

        lax.fori_loop(0, depth, scaled, 0)
        return copy

    def step(turn, carry):
        def send_q():
            for copy in z_copies(Q, 2):
                copy.start()

        def send_s():
            @pl.when(turn < STEPS - 1)
            def _():
                for copy in z_copies(S, 0):
                    copy.start()

        def send_gs():
            @pl.when(turn < STEPS - 1)
            def _():
                g_copy(GS, OS, 0).start()

        def couplings():
            @pl.when(turn == 0)
            def _():
                g_copy(GJ.at[2], OJ, 2).wait()

        stage(S, GS, OS, 0, predict, predict_ghost, send_q, lambda: g_copy(GQ, OQ, 1).start(), couplings)

        @pl.when(turn == 2)
        def _():
            pltpu.make_async_copy(out, mid_ref, osem.at[0]).wait()

        stage(Q, GQ, OQ, 1, correct, correct_ghost, send_s, send_gs)

        @pl.when(turn == 1)
        def _():
            publish(mid_ref, osem.at[0]).start()

        return carry

    lax.fori_loop(0, STEPS, step, 0)
    final = publish(end_ref, osem.at[0])
    final.start()
    final.wait()


def evolve(polar_angle, azimuth, classes, exchange_table):
    depth, wide, lanes = polar_angle.shape
    sizes = (lax.axis_size("gx"), lax.axis_size("gy"), lax.axis_size("gz"))
    assert sizes[2] == 2 and depth * 2 * HALO == lanes
    ext = wide + 2 * HALO
    f32, i32 = jnp.float32, jnp.int32
    out = jax.ShapeDtypeStruct((3, depth, wide, lanes), f32)
    hbm = pl.BlockSpec(memory_space=pltpu.HBM)
    anywhere = pl.BlockSpec(memory_space=pl.ANY)
    V = pltpu.VMEM
    D = pltpu.SemaphoreType.DMA
    return pl.pallas_call(
        functools.partial(evolve_kernel, sizes),
        out_shape=(out, out),
        in_specs=[hbm, hbm, hbm, pl.BlockSpec(memory_space=pltpu.SMEM)],
        out_specs=(anywhere, anywhere),
        scratch_shapes=[
            V((depth, wide, lanes), f32), V((depth, wide, lanes), f32), V((5, depth, wide, lanes), i32),
            V((3, depth + 2, ext, lanes), f32), V((3, depth + 2, ext, lanes), f32),
            V((4, depth + 1, ext, lanes), f32),
            V((3, ext, lanes), f32), V((3, ext, lanes), f32), V((4, ext, lanes), f32),
            V((3, ext, lanes), f32), V((3, ext, lanes), f32), V((ext, lanes), f32),
            V((2, depth, HALO, lanes), f32), V((2, depth, HALO, lanes), f32),
            V((4, depth, HALO, lanes), i32), V((4, depth, HALO, lanes), i32),
            V((5, wide, lanes), f32), V((5, ext, lanes), f32), V((5, ext, lanes), f32),
            V((3, depth, wide, lanes), f32),
            D((8,)), D((8,)), D((6,)), D((6,)), D((4,)), D((4,)), D((3,)), D((3,)), D((1,)), D((5,)),
        ],
        compiler_params=pltpu.CompilerParams(collective_id=0, has_side_effects=True, vmem_limit_bytes=65200000),
        name="evolve",
    )(polar_angle, azimuth, classes, exchange_table)


def phase_table(wave_count, total_length):
    index = np.arange(total_length)[:, None] * np.arange(wave_count)[None, :] % total_length
    phase = index * (2.0 * math.pi / total_length)
    return np.cos(phase).astype(np.float32), np.sin(phase).astype(np.float32)


def exact_dot(a, b):
    return jnp.dot(a, b, precision=lax.Precision.HIGHEST, preferred_element_type=jnp.float32)


def modes_kernel(sizes, scale, mid_ref, end_ref, x_in, y_in, cos_ref, sin_ref, out_ref,
                 x_ref, y_ref, T, R, Z, D, DR, E, F, zs, zr, xs, xr, ys, yr, fs, fr, isem):
    nx, ny, nz = sizes
    depth, wide, lanes = mid_ref.shape[1:]
    owned = D.shape[2]
    half = KX // nz
    me_x, me_y, me_z = lax.axis_index("gx"), lax.axis_index("gy"), lax.axis_index("gz")
    peers_x = [{"gx": lax.rem(me_x + o, nx)} for o in range(1, nx)]
    peers_y = [{"gy": lax.rem(me_y + o, ny)} for o in range(1, ny)]
    twin = {"gz": 1 - me_z}
    fetches = [
        pltpu.make_async_copy(x_in.at[me_x], x_ref, isem.at[0]),
        pltpu.make_async_copy(y_in.at[me_y], y_ref, isem.at[1]),
    ]
    for copy in fetches:
        copy.start()

    barrier = pltpu.get_barrier_semaphore()
    for who in peers_x + peers_y + [twin]:
        pl.semaphore_signal(barrier, inc=1, device_id=who, device_id_type=MESH)
    pl.semaphore_wait(barrier, nx + ny - 1)

    def remote(src, dst, send, recv, who):
        return pltpu.make_async_remote_copy(
            src_ref=src, dst_ref=dst, send_sem=send, recv_sem=recv, device_id=who, device_id_type=MESH
        )

    lane = lax.broadcasted_iota(jnp.int32, (half, 4 * KY), 1)
    cosine_lane = (lane // KY) % 2 == 0
    for copy in fetches:
        copy.wait()
    table = x_ref[...]
    swaps, x_copies, y_copies, shares = [], [], [], []

    def transform(c):
        for z in range(depth):
            for turn, ref in enumerate((mid_ref, end_ref)):
                along_x = exact_dot(table, ref[c, z])
                T[pl.ds(z * KX, KX), pl.ds(2 * lanes * turn, lanes)] = along_x[:KX]
                T[pl.ds(z * KX, KX), pl.ds(2 * lanes * turn + lanes, lanes)] = along_x[KX:]
        parts = exact_dot(T[...], y_ref[...]).reshape(depth, nz, half, 4 * KY)
        for h in range(nz):
            R[h, c] = parts[:, h]
        swaps.append(remote(R.at[1 - me_z, c], Z.at[c], zs.at[c], zr.at[c], twin))
        swaps[c].start()

    def waves(c):
        swaps[c].wait()
        ones, twos = [], []
        for z in range(nz * depth):
            own = R[me_z, c, z] if z < depth else Z[c, z - depth]
            ones.append(own)
            twos.append(jnp.where(cosine_lane, -pltpu.roll(own, 3 * KY, 1), pltpu.roll(own, KY, 1)))

        def block_of(block, carry):
            for k in range(owned):
                total = None
                for z in range(nz * depth):
                    where_z = me_z * depth + z if z < depth else (1 - me_z) * depth + z - depth
                    wave = block * owned + k
                    term = cos_ref[wave, where_z] * ones[z] + sin_ref[wave, where_z] * twos[z]
                    total = term if total is None else total + term
                D[c, block, k] = total
            return carry

        lax.fori_loop(0, nx, block_of, 0)
        x_copies.append([
            remote(D.at[c, lax.rem(me_x + o, nx)], DR.at[c, o - 1], xs.at[c, o - 1], xr.at[c, o - 1], peers_x[o - 1])
            for o in range(1, nx)
        ])
        for copy in reversed(x_copies[c]):
            copy.start()

    def sum_x(c):
        for copy in x_copies[c]:
            copy.wait()
        total = D[c, me_x]
        for o in range(1, nx):
            total = total + DR[c, o - 1]
        E[c, me_y] = total
        y_copies.append([
            remote(E.at[c, me_y], E.at[c, me_y], ys.at[c, o - 1], yr.at[c, o - 1], peers_y[o - 1])
            for o in range(1, ny)
        ])
        for copy in y_copies[c]:
            copy.start()

    def sum_y(c):
        for copy in y_copies[c]:
            copy.wait()
        total = E[c, 0]
        for o in range(1, ny):
            total = total + E[c, o]
        F[c, me_z] = total * jnp.where(cosine_lane, scale, -scale)
        shares.append(remote(F.at[c, me_z], F.at[c, me_z], fs.at[c], fr.at[c], twin))
        shares[c].start()

    transform(0)
    transform(1)
    waves(0)
    transform(2)
    waves(1)
    waves(2)
    sum_x(0)
    sum_x(1)
    sum_y(0)
    sum_x(2)
    sum_y(1)
    sum_y(2)
    for c in range(3):
        shares[c].wait()
        out_ref[:, :, c] = F[c]


def modes(spin_mid, spin_end):
    depth, wide, lanes = spin_mid.shape[1:]
    sizes = nx, ny, nz = (lax.axis_size("gx"), lax.axis_size("gy"), lax.axis_size("gz"))
    total_z = depth * nz
    owned = total_z // nx
    half = KX // nz
    f32 = jnp.float32
    x_cos, x_sin = phase_table(KX, wide * nx)
    y_cos, y_sin = phase_table(KY, lanes * ny)
    z_cos, z_sin = phase_table(total_z, total_z)
    x_full = np.concatenate([x_cos, x_sin], 1).reshape(nx, wide, 2 * KX).transpose(0, 2, 1)
    y_pair = np.stack([
        np.concatenate([y_cos, y_sin], 1).reshape(ny, lanes, 2 * KY),
        np.concatenate([-y_sin, y_cos], 1).reshape(ny, lanes, 2 * KY),
    ], 1).reshape(ny, 2 * lanes, 2 * KY)
    y_full = np.zeros((ny, 4 * lanes, 4 * KY), np.float32)
    y_full[:, : 2 * lanes, : 2 * KY] = y_pair
    y_full[:, 2 * lanes :, 2 * KY :] = y_pair
    scale = float(wide * nx * lanes * ny * total_z) ** -0.5
    vmem = pl.BlockSpec(memory_space=pltpu.VMEM)
    smem = pl.BlockSpec(memory_space=pltpu.SMEM)
    hbm = pl.BlockSpec(memory_space=pltpu.HBM)
    V, DMA = pltpu.VMEM, pltpu.SemaphoreType.DMA
    width = 4 * KY
    out = pl.pallas_call(
        functools.partial(modes_kernel, sizes, scale),
        out_shape=jax.ShapeDtypeStruct((nz, owned, 3, half, width), f32),
        in_specs=[vmem, vmem, hbm, hbm, smem, smem],
        out_specs=vmem,
        scratch_shapes=[
            V((2 * KX, wide), f32), V((4 * lanes, width), f32),
            V((depth * KX, 4 * lanes), f32), V((nz, 3, depth, half, width), f32),
            V((3, depth, half, width), f32), V((3, nx, owned, half, width), f32),
            V((3, nx - 1, owned, half, width), f32), V((3, ny, owned, half, width), f32),
            V((3, nz, owned, half, width), f32),
            DMA((3,)), DMA((3,)), DMA((3, nx - 1)), DMA((3, nx - 1)), DMA((3, ny - 1)), DMA((3, ny - 1)),
            DMA((3,)), DMA((3,)), DMA((2,)),
        ],
        compiler_params=pltpu.CompilerParams(collective_id=1, has_side_effects=True, vmem_limit_bytes=32 * 1024 * 1024),
        name="modes",
    )(spin_mid, spin_end, jnp.asarray(x_full), jnp.asarray(y_full), jnp.asarray(z_cos.T), jnp.asarray(z_sin.T))
    out = out.reshape(nz, owned, 3, half, 2, 2, KY).transpose(4, 1, 5, 2, 0, 3, 6)
    return out.reshape(2, owned, -1)


def body(polar_angle, azimuth, classes, exchange_table):
    spin_mid, spin_end = evolve(polar_angle, azimuth, classes, exchange_table)
    both = modes(spin_mid, spin_end)
    return (spin_end, both[0], both[1])


def solution(mesh):
    return jax.shard_map(
        body,
        mesh=mesh,
        in_specs=(
            P("gz", ("groups", "gx"), "gy"),
            P("gz", ("groups", "gx"), "gy"),
            P(None, "gz", ("groups", "gx"), "gy"),
            P(),
        ),
        out_specs=(
            P(None, "gz", ("groups", "gx"), "gy"),
            P(("groups", "gx"), None),
            P(("groups", "gx"), None),
        ),
        check_vma=False,
    )
```

time: 72.2 us -> 60.5 us (0.84)
  Pallas kernels: 65.2 us -> 53.6 us
    pallas_call x1, Pallas kernels: 43.1 us -> 31.7 us  [evolve(): pl.pallas_call(functools.partial(evolve_kernel, sizes), out_shape=(out, o...]
where the time goes in v1:
time: 60.5 us; the launch traced here: 60.3 us
  Pallas kernels  53.6 us (89%)
  local copies, waits for them, and re-layouts  6 us (10%)
  between operations  0.76 us (1%)
    pallas_call x1, Pallas kernels, evolve(): pl.pallas_call(functools.partial(evolve_kernel, sizes), out_shape=(out, o...  31.7 us
    pallas_call x1, Pallas kernels, modes(): pl.pallas_call(functools.partial(modes_kernel, sizes, scale), out_shape=j...  21.9 us
    unnamed x15, local copies, waits for them, and re-layouts  3.17 us
    squeeze x2, local copies, waits for them, and re-layouts, body(): return (spin_end, both[0], both[1])  1.7 us

profile of v1, /device:TPU:0, one launch (start us, length us, event | category | flops | bytes accessed | tf_op | source)
XLA Modules:
  0.0 60.3 jit_solution(18429102667018300707)
XLA Ops:
  0.6 0.0 copy-start.5
  0.6 0.0 copy-start.6
  0.7 0.0 copy-start.3
  0.7 0.0 copy-start.4
  0.7 31.7 %evolve.1 = (f32[3,8,64,128]{3,2,1,0:T(8,128)}, f32[3,8,64,128]{3,2,1,0:T(8,128)}) custom-call(f32[8,64,128]{2,1,0:T(8,128)} %polar_in.1, f32[8,64,128]{2,1,0:T(8,128)} %azimuth_in.1, s32[6,8,64,128]{3,2,1,0:T(8,128)} %classes_in.1, f32[8]{0:T(128)} %table_ref.1), custom_call_target="tpu_custom_call" | custom-call | tf_op jit(solution)/shard_map/evolve/pallas_call | solution.py:377
  32.4 0.0 copy-done.5
  32.4 0.0 copy-done.6
  32.4 0.0 copy-done.3
  32.4 0.0 copy-done.4
  32.4 0.0 copy-start
  32.4 1.1 %copy-done = f32[3,8,64,128]{3,2,1,0:T(8,128)S(1)} copy-done((f32[3,8,64,128]{3,2,1,0:T(8,128)S(1)}, f32[3,8,64,128]{3,2,1,0:T(8,128)}, u32[]{:S(2)}) %copy-start) | copy-done | bytes 786456
  33.6 0.0 copy-start.2
  33.6 1.1 %copy-done.2 = f32[3,8,64,128]{3,2,1,0:T(8,128)S(1)} copy-done((f32[3,8,64,128]{3,2,1,0:T(8,128)S(1)}, f32[3,8,64,128]{3,2,1,0:T(8,128)}, u32[]{:S(2)}) %copy-start.2) | copy-done | bytes 786456
  34.7 21.9 %modes.1 = f32[2,4,3,16,128]{4,3,2,1,0:T(8,128)S(1)} custom-call(f32[3,8,64,128]{3,2,1,0:T(8,128)S(1)} %copy-done.2, f32[3,8,64,128]{3,2,1,0:T(8,128)S(1)} %copy-done, f32[4,64,64]{2,1,0:T(8,128)S(1)} %copy-done.4, f32[2,512,128]{2,1,0:T(8,128)S(1)} %copy-done.3, f32[16,16]{1,0:T(8,128)S(1)} %copy-done.6, f32[16,16]{1,0:T(8,128)S(1)} %copy-done.5), custom_call_target="tpu_custom_call" | custom-call | tf_op jit(solution)/shard_map/modes/pallas_call | solution.py:547
  56.6 0.6 %reshape.14 = f32[2,4,3,16,2,2,32]{6,5,4,3,2,1,0:T(2,128)S(1)} reshape(f32[2,4,3,16,128]{4,3,2,1,0:T(8,128)S(1)} %modes.1) | data formatting | bytes 393216 | tf_op jit(solution)/shard_map/reshape | solution.py:564
  57.2 0.4 fusion
  57.6 0.0 copy-start.1
  57.7 0.9 %squeeze.7 = f32[4,6144]{1,0:T(4,128)} reshape(f32[1,4,2,3,2,16,32]{6,5,4,3,2,1,0:T(8,128)S(1)} %copy.12) | data formatting | bytes 196608 | tf_op jit(solution)/shard_map/squeeze | solution.py:571
  58.6 0.9 %squeeze.6 = f32[4,6144]{1,0:T(4,128)} reshape(f32[1,4,2,3,2,16,32]{6,5,4,3,2,1,0:T(8,128)S(1)} %copy.11) | data formatting | bytes 196608 | tf_op jit(solution)/shard_map/squeeze | solution.py:571
  59.4 0.0 copy-done.1
  59.4 0.9 %copy.14 = f32[3,8,64,128]{3,2,1,0:T(8,128)} copy(f32[3,8,64,128]{3,2,1,0:T(8,128)S(1)} %copy-done.1) | data formatting | bytes 1572864
  (2 shorter events, 0.1 us)
Async XLA Ops:
  0.6 31.7 %copy-start.5 = (f32[16,16]{1,0:T(8,128)S(1)}, f32[16,16]{1,0:T(8,128)}, u32[]{:S(2)}) copy-start(f32[16,16]{1,0:T(8,128)} %constant.11.clone.sin_ref) | copy-start | bytes 3076
  0.6 31.7 %copy-start.6 = (f32[16,16]{1,0:T(8,128)S(1)}, f32[16,16]{1,0:T(8,128)}, u32[]{:S(2)}) copy-start(f32[16,16]{1,0:T(8,128)} %constant.10.clone.cos_ref) | copy-start | bytes 3076
  0.7 31.7 %copy-start.3 = (f32[2,512,128]{2,1,0:T(8,128)S(1)}, f32[2,512,128]{2,1,0:T(8,128)}, u32[]{:S(2)}) copy-start(f32[2,512,128]{2,1,0:T(8,128)} %constant.9.clone.y_in) | copy-start | bytes 1572868
  0.7 31.7 %copy-start.4 = (f32[4,64,64]{2,1,0:T(8,128)S(1)}, f32[4,64,64]{2,1,0:T(8,128)}, u32[]{:S(2)}) copy-start(f32[4,64,64]{2,1,0:T(8,128)} %constant.8.clone.x_in) | copy-start | bytes 196612
  32.4 1.1 %copy-start = (f32[3,8,64,128]{3,2,1,0:T(8,128)S(1)}, f32[3,8,64,128]{3,2,1,0:T(8,128)}, u32[]{:S(2)}) copy-start(f32[3,8,64,128]{3,2,1,0:T(8,128)} %get-tuple-element.12.end_ref) | copy-start | bytes 2359300
  33.6 1.1 %copy-start.2 = (f32[3,8,64,128]{3,2,1,0:T(8,128)S(1)}, f32[3,8,64,128]{3,2,1,0:T(8,128)}, u32[]{:S(2)}) copy-start(f32[3,8,64,128]{3,2,1,0:T(8,128)} %get-tuple-element.6.mid_ref) | copy-start | bytes 2359300
  57.6 1.8 %copy-start.1 = (f32[3,8,64,128]{3,2,1,0:T(8,128)S(1)}, f32[3,8,64,128]{3,2,1,0:T(8,128)}, u32[]{:S(2)}) copy-start(f32[3,8,64,128]{3,2,1,0:T(8,128)} %get-tuple-element.12.end_ref) | copy-start | bytes 2359300

commit v2 on v1

--- a/solution.py
+++ b/solution.py
@@ -54,10 +54,11 @@
     return s1 * w2 - s2 * w1, s2 * w0 - s0 * w2, s0 * w1 - s1 * w0
 
 
-def evolve_kernel(sizes, polar_in, azimuth_in, classes_in, table_ref, mid_ref, end_ref,
+def evolve_kernel(sizes, polar_in, azimuth_in, classes_in, y_in, x_in, z_in, table_ref, end_ref, mid_out, end_out,
                   polar_ref, azimuth_ref, classes_ref, S, Q, J, GS, GQ, GJ, OS, OQ, OJ,
                   low, high, lowk, highk, pack, left_pack, right_pack, out,
-                  xs, xr, ys, yr, zs, zr, gs, gr, osem, isem):
+                  y_table, x_table, z_table, along_y, waves_xy, planes, twin_planes, sums, peer_sums, rows_sum, whole,
+                  xs, xr, ys, yr, zs, zr, gs, gr, osem, isem, ts, tr, ps, pr, qs, qr, fs, fr):
     nx, ny, nz = sizes
     depth, wide, lanes = polar_ref.shape
     ext = wide + 2 * HALO
@@ -81,10 +82,17 @@
         pltpu.make_async_copy(classes_in.at[4], classes_ref.at[3], isem.at[3]),
         pltpu.make_async_copy(classes_in.at[5, 0], classes_ref.at[4, 0], isem.at[4]),
     ]
-    for copy in fetches:
+    tables = [
+        pltpu.make_async_copy(y_in.at[me_y], y_table, isem.at[5]),
+        pltpu.make_async_copy(x_in.at[me_x], x_table, isem.at[6]),
+        pltpu.make_async_copy(z_in.at[me_z], z_table, isem.at[7]),
+    ]
+    for copy in fetches + tables:
         copy.start()
+    peers_x = [at("gx", me_x, nx, o) for o in range(1, nx)]
+    peers_y = [at("gy", me_y, ny, o) for o in range(1, ny)]
     barrier = pltpu.get_barrier_semaphore()
-    friends = [x_left, x_right, z_up] + sides + [{**x, **y} for x in (x_left, x_right) for y in sides]
+    friends = peers_x + peers_y + [z_up] + [{**x, **y} for x in (x_left, x_right) for y in sides]
     for who in friends:
         pl.semaphore_signal(barrier, inc=1, device_id=who, device_id_type=MESH)
     pl.semaphore_wait(barrier, len(friends))
@@ -290,9 +298,7 @@
         for c in range(3):
             GS[c, rows, :] = 0.5 * (GS[c, rows, :] + (spin[c] - change[c]))
 
-    def stage(F, G, O, base, finish, finish_ghost, send_main, send_ghost, first=None):
-        every = range(tiles)
-
+    def stage(F, G, O, base, finish, finish_ghost, send_main, send_ghost, first=None, every=range(tiles)):
         def inside(i, carry):
             plane(F, G, 2 * i + 1, finish, every)
             plane(F, G, 2 * i + 2, finish, every)
@@ -305,80 +311,232 @@
         plane(F, G, depth - 1, finish, every)
         send_main()
         g_copy(G, O, base).wait()
+        if finish_ghost is None:
+            return
         if first is not None:
             first()
         ghost_pass(F, G, O, finish_ghost)
         send_ghost()
 
-    def publish(target, sem):
-        copy = pltpu.make_async_copy(out, target, sem)
-
-        def scaled(z, carry):
-            for c in range(3):
-                for r in range(inner):
-                    out[c, z, pl.ds(8 * r, 8), :] = S[c, z + 1, pl.ds(HALO + 8 * r, 8), :] * (1.0 / damping)
-            return carry
-
-        lax.fori_loop(0, depth, scaled, 0)
-        return copy
+    def split(value):
+        big = value.astype(jnp.bfloat16)
+        return big, (value - big.astype(jnp.float32)).astype(jnp.bfloat16)
+
+    def dot(a, b):
+        return jnp.dot(a, b, preferred_element_type=jnp.float32)
+
+    half = KX // nz
+    quad = lanes // KY
+
+    def transform(f, c):
+        for z in range(depth):
+            big, small = split(S[c, z + 1, pl.ds(HALO, wide), :])
+            along_y[pl.ds(z * wide, wide), pl.ds(0, lanes)] = big
+            along_y[pl.ds(z * wide, wide), pl.ds(lanes, lanes)] = small
+        both = dot(along_y[...], y_table[...])
+        both = both[:, :lanes] + both[:, lanes:]
+        for z in range(0, depth, 2):
+            parts = []
+            for i in (z, z + 1):
+                big, small = split(both[i * wide : (i + 1) * wide])
+                parts.append(jnp.concatenate([big, small, big, small], 0))
+            along_x = dot(x_table[...], jnp.concatenate(parts, 1))
+            for i in range(2):
+                mine = along_x[:, i * lanes : (i + 1) * lanes]
+                waves_xy[pl.ds((z + i) * KX, KX), :] = mine[:KX] + pltpu.roll(mine[KX:], lanes // 2, 1)
+        slot = lane // KY
+        for h in range(nz):
+            for j in range(half // quad):
+                loads = [waves_xy[pl.ds(h * half + j * quad + k, depth, stride=KX), :] for k in range(quad)]
+                for p in range(2):
+                    total = None
+                    for k, value in enumerate(loads):
+                        turn = (k - p) % quad * KY
+                        value = pltpu.roll(value, turn, 1) if turn else value
+                        total = value if total is None else jnp.where(slot == k, value, total)
+                    planes[f, h, c, pl.ds(p * depth, depth), pl.ds(j * lanes, lanes)] = total
+
+    def swap(f, c):
+        return remote(planes.at[f, 1 - me_z, c], twin_planes.at[f, c], ts.at[f, c], tr.at[f, c], z_up)
+
+    def waves(f, c):
+        stacked = jnp.concatenate([planes[f, me_z, c], twin_planes[f, c]], 0)
+        big, small = split(stacked)
+        result = dot(z_table[...], jnp.concatenate([big, small, big, small], 0))
+        for b in range(nx):
+            sums[f, c, b] = result[8 * b : 8 * b + 8]
+
+    def x_sends(f, c):
+        return [
+            remote(sums.at[f, c, lax.rem(me_x + o, nx)], peer_sums.at[f, c, o - 1], ps.at[f, c, o - 1],
+                   pr.at[f, c, o - 1], peers_x[o - 1])
+            for o in range(1, nx)
+        ]
+
+    def y_sends(f, c):
+        return [
+            remote(rows_sum.at[f, c, me_y], rows_sum.at[f, c, me_y], qs.at[f, c, o - 1], qr.at[f, c, o - 1],
+                   peers_y[o - 1])
+            for o in range(1, ny)
+        ]
+
+    def share(f, c):
+        return remote(whole.at[f, c, me_z], whole.at[f, c, me_z], fs.at[f, c], fr.at[f, c], z_up)
+
+    def local_part(f):
+        for c in range(3):
+            transform(f, c)
+            swap(f, c).start()
+
+    def wave_part(f):
+        for c in range(3):
+            swap(f, c).wait()
+            waves(f, c)
+            for copy in reversed(x_sends(f, c)):
+                copy.start()
+
+    def x_part(f):
+        for c in range(3):
+            for copy in x_sends(f, c):
+                copy.wait()
+            total = sums[f, c, me_x]
+            for o in range(1, nx):
+                total = total + peer_sums[f, c, o - 1]
+            rows_sum[f, c, me_y] = total
+            for copy in y_sends(f, c):
+                copy.start()
+
+    def y_part(f):
+        for c in range(3):
+            for copy in y_sends(f, c):
+                copy.wait()
+            total = rows_sum[f, c, 0]
+            for o in range(1, ny):
+                total = total + rows_sum[f, c, o]
+            whole[f, c, me_z] = total
+            share(f, c).start()
+
+    def last_part(f, target):
+        owned = target.shape[0]
+        for c in range(3):
+            share(f, c).wait()
+            for h in range(nz):
+                for p in range(2):
+                    start = (p * 3 + c) * KX * KY + h * half * KY
+                    target[:, pl.ds(start, half * KY)] = whole[f, c, h, pl.ds(p * owned, owned), :]
+
+    def send_q():
+        for copy in z_copies(Q, 2):
+            copy.start()
+
+    def send_s():
+        for copy in z_copies(S, 0):
+            copy.start()
+
+    def predict_stage(first=None):
+        stage(S, GS, OS, 0, predict, predict_ghost, send_q, lambda: g_copy(GQ, OQ, 1).start(), first)
 
     def step(turn, carry):
-        def send_q():
-            for copy in z_copies(Q, 2):
-                copy.start()
-
-        def send_s():
-            @pl.when(turn < STEPS - 1)
-            def _():
-                for copy in z_copies(S, 0):
-                    copy.start()
-
-        def send_gs():
-            @pl.when(turn < STEPS - 1)
-            def _():
-                g_copy(GS, OS, 0).start()
-
         def couplings():
             @pl.when(turn == 0)
             def _():
                 g_copy(GJ.at[2], OJ, 2).wait()
 
-        stage(S, GS, OS, 0, predict, predict_ghost, send_q, lambda: g_copy(GQ, OQ, 1).start(), couplings)
-
-        @pl.when(turn == 2)
+        predict_stage(couplings)
+        stage(Q, GQ, OQ, 1, correct, correct_ghost, send_s, lambda: g_copy(GS, OS, 0).start())
+
+        @pl.when(turn == STEPS // 2 - 1)
         def _():
-            pltpu.make_async_copy(out, mid_ref, osem.at[0]).wait()
-
-        stage(Q, GQ, OQ, 1, correct, correct_ghost, send_s, send_gs)
-
-        @pl.when(turn == 1)
+            local_part(0)
+
+        @pl.when(turn == STEPS // 2)
         def _():
-            publish(mid_ref, osem.at[0]).start()
-
-        return carry
-
-    lax.fori_loop(0, STEPS, step, 0)
-    final = publish(end_ref, osem.at[0])
+            wave_part(0)
+
+        return carry
+
+    for copy in tables:
+        copy.wait()
+    lax.fori_loop(0, STEPS - 1, step, 0)
+    predict_stage()
+    stage(Q, GQ, OQ, 1, correct, None, lambda: None, None, every=range(1, tiles - 1))
+    local_part(1)
+
+    def scaled(z, carry):
+        for c in range(3):
+            for r in range(inner):
+                out[c, z, pl.ds(8 * r, 8), :] = S[c, z + 1, pl.ds(HALO + 8 * r, 8), :] * (1.0 / damping)
+        return carry
+
+    lax.fori_loop(0, depth, scaled, 0)
+    final = pltpu.make_async_copy(out, end_ref, osem.at[0])
     final.start()
+    wave_part(1)
+    x_part(0)
+    y_part(0)
+    last_part(0, mid_out)
+    x_part(1)
+    y_part(1)
+    last_part(1, end_out)
     final.wait()
+
+
+def phase_table(wave_count, total_length):
+    index = np.arange(total_length)[:, None] * np.arange(wave_count)[None, :] % total_length
+    phase = index * (2.0 * math.pi / total_length)
+    return np.cos(phase), np.sin(phase)
+
+
+def halves(table):
+    big = table.astype(jnp.bfloat16)
+    small = (table - big.astype(np.float64)).astype(jnp.bfloat16)
+    return big, small
+
+
+def wave_tables(depth, wide, lanes, nx, ny, nz):
+    total_z = depth * nz
+    owned = total_z // nx
+    x_cos, x_sin = phase_table(KX, wide * nx)
+    y_cos, y_sin = phase_table(KY, lanes * ny)
+    z_cos, z_sin = phase_table(total_z, total_z)
+    big, small = halves(np.concatenate([y_cos, y_sin, -y_sin, y_cos], 1).reshape(ny, lanes, 4 * KY))
+    row = np.concatenate([big, small], 2)
+    y_all = np.concatenate([row, row], 1)
+    big, small = halves(np.concatenate([x_cos, x_sin], 1).reshape(nx, wide, 2 * KX).transpose(0, 2, 1))
+    x_all = np.concatenate([big, big, small, small], 2)
+    scale = float(wide * nx * lanes * ny * total_z) ** -0.5 / damping
+    z_full = np.zeros((nz, nx, 8, nz, 2, depth))
+    for first in range(nz):
+        for place in range(nz):
+            where = (first + place) % nz * depth + np.arange(depth)
+            for p, (even, odd) in enumerate(((z_cos, -z_sin), (-z_sin, -z_cos))):
+                for part, table in enumerate((even, odd)):
+                    values = table[where].T.reshape(nx, owned, depth) * scale
+                    z_full[first, :, p * owned : (p + 1) * owned, place, part] = values
+    big, small = halves(z_full.reshape(nz, nx * 8, nz * 2 * depth))
+    z_all = np.concatenate([big, big, small, small], 2)
+    return jnp.asarray(y_all), jnp.asarray(x_all), jnp.asarray(z_all)
 
 
 def evolve(polar_angle, azimuth, classes, exchange_table):
     depth, wide, lanes = polar_angle.shape
-    sizes = (lax.axis_size("gx"), lax.axis_size("gy"), lax.axis_size("gz"))
-    assert sizes[2] == 2 and depth * 2 * HALO == lanes
+    sizes = nx, ny, nz = (lax.axis_size("gx"), lax.axis_size("gy"), lax.axis_size("gz"))
+    owned = depth * nz // nx
+    half = KX // nz
+    assert nz == 2 and depth * 2 * HALO == lanes and lanes == 4 * KY and 0 < 2 * owned <= 8
     ext = wide + 2 * HALO
-    f32, i32 = jnp.float32, jnp.int32
-    out = jax.ShapeDtypeStruct((3, depth, wide, lanes), f32)
+    f32, i32, b16 = jnp.float32, jnp.int32, jnp.bfloat16
     hbm = pl.BlockSpec(memory_space=pltpu.HBM)
     anywhere = pl.BlockSpec(memory_space=pl.ANY)
+    vmem = pl.BlockSpec(memory_space=pltpu.VMEM)
     V = pltpu.VMEM
     D = pltpu.SemaphoreType.DMA
+    modes = jax.ShapeDtypeStruct((owned, 6 * KX * KY), f32)
     return pl.pallas_call(
         functools.partial(evolve_kernel, sizes),
-        out_shape=(out, out),
-        in_specs=[hbm, hbm, hbm, pl.BlockSpec(memory_space=pltpu.SMEM)],
-        out_specs=(anywhere, anywhere),
+        out_shape=(jax.ShapeDtypeStruct((3, depth, wide, lanes), f32), modes, modes),
+        in_specs=[hbm] * 6 + [pl.BlockSpec(memory_space=pltpu.SMEM)],
+        out_specs=(anywhere, vmem, vmem),
         scratch_shapes=[
             V((depth, wide, lanes), f32), V((depth, wide, lanes), f32), V((5, depth, wide, lanes), i32),
             V((3, depth + 2, ext, lanes), f32), V((3, depth + 2, ext, lanes), f32),
@@ -389,191 +547,23 @@
             V((4, depth, HALO, lanes), i32), V((4, depth, HALO, lanes), i32),
             V((5, wide, lanes), f32), V((5, ext, lanes), f32), V((5, ext, lanes), f32),
             V((3, depth, wide, lanes), f32),
-            D((8,)), D((8,)), D((6,)), D((6,)), D((4,)), D((4,)), D((3,)), D((3,)), D((1,)), D((5,)),
+            V((2 * lanes, 2 * lanes), b16), V((2 * KX, 4 * wide), b16), V((nx * 8, 8 * nz * depth), b16),
+            V((depth * wide, 2 * lanes), b16), V((depth * KX, lanes), f32),
+            V((2, nz, 3, 2 * depth, half * KY), f32), V((2, 3, 2 * depth, half * KY), f32),
+            V((2, 3, nx, 8, half * KY), f32), V((2, 3, nx - 1, 8, half * KY), f32),
+            V((2, 3, ny, 8, half * KY), f32), V((2, 3, nz, 8, half * KY), f32),
+            D((8,)), D((8,)), D((6,)), D((6,)), D((4,)), D((4,)), D((3,)), D((3,)), D((1,)), D((8,)),
+            D((2, 3)), D((2, 3)), D((2, 3, nx - 1)), D((2, 3, nx - 1)), D((2, 3, ny - 1)), D((2, 3, ny - 1)),
+            D((2, 3)), D((2, 3)),
         ],
-        compiler_params=pltpu.CompilerParams(collective_id=0, has_side_effects=True, vmem_limit_bytes=65200000),
+        compiler_params=pltpu.CompilerParams(collective_id=0, has_side_effects=True, vmem_limit_bytes=60000000),
         name="evolve",
-    )(polar_angle, azimuth, classes, exchange_table)
-
-
-def phase_table(wave_count, total_length):
-    index = np.arange(total_length)[:, None] * np.arange(wave_count)[None, :] % total_length
-    phase = index * (2.0 * math.pi / total_length)
-    return np.cos(phase).astype(np.float32), np.sin(phase).astype(np.float32)
-
-
-def exact_dot(a, b):
-    return jnp.dot(a, b, precision=lax.Precision.HIGHEST, preferred_element_type=jnp.float32)
-
-
-def modes_kernel(sizes, scale, mid_ref, end_ref, x_in, y_in, cos_ref, sin_ref, out_ref,
-                 x_ref, y_ref, T, R, Z, D, DR, E, F, zs, zr, xs, xr, ys, yr, fs, fr, isem):
-    nx, ny, nz = sizes
-    depth, wide, lanes = mid_ref.shape[1:]
-    owned = D.shape[2]
-    half = KX // nz
-    me_x, me_y, me_z = lax.axis_index("gx"), lax.axis_index("gy"), lax.axis_index("gz")
-    peers_x = [{"gx": lax.rem(me_x + o, nx)} for o in range(1, nx)]
-    peers_y = [{"gy": lax.rem(me_y + o, ny)} for o in range(1, ny)]
-    twin = {"gz": 1 - me_z}
-    fetches = [
-        pltpu.make_async_copy(x_in.at[me_x], x_ref, isem.at[0]),
-        pltpu.make_async_copy(y_in.at[me_y], y_ref, isem.at[1]),
-    ]
-    for copy in fetches:
-        copy.start()
-
-    barrier = pltpu.get_barrier_semaphore()
-    for who in peers_x + peers_y + [twin]:
-        pl.semaphore_signal(barrier, inc=1, device_id=who, device_id_type=MESH)
-    pl.semaphore_wait(barrier, nx + ny - 1)
-
-    def remote(src, dst, send, recv, who):
-        return pltpu.make_async_remote_copy(
-            src_ref=src, dst_ref=dst, send_sem=send, recv_sem=recv, device_id=who, device_id_type=MESH
-        )
-
-    lane = lax.broadcasted_iota(jnp.int32, (half, 4 * KY), 1)
-    cosine_lane = (lane // KY) % 2 == 0
-    for copy in fetches:
-        copy.wait()
-    table = x_ref[...]
-    swaps, x_copies, y_copies, shares = [], [], [], []
-
-    def transform(c):
-        for z in range(depth):
-            for turn, ref in enumerate((mid_ref, end_ref)):
-                along_x = exact_dot(table, ref[c, z])
-                T[pl.ds(z * KX, KX), pl.ds(2 * lanes * turn, lanes)] = along_x[:KX]
-                T[pl.ds(z * KX, KX), pl.ds(2 * lanes * turn + lanes, lanes)] = along_x[KX:]
-        parts = exact_dot(T[...], y_ref[...]).reshape(depth, nz, half, 4 * KY)
-        for h in range(nz):
-            R[h, c] = parts[:, h]
-        swaps.append(remote(R.at[1 - me_z, c], Z.at[c], zs.at[c], zr.at[c], twin))
-        swaps[c].start()
-
-    def waves(c):
-        swaps[c].wait()
-        ones, twos = [], []
-        for z in range(nz * depth):
-            own = R[me_z, c, z] if z < depth else Z[c, z - depth]
-            ones.append(own)
-            twos.append(jnp.where(cosine_lane, -pltpu.roll(own, 3 * KY, 1), pltpu.roll(own, KY, 1)))
-
-        def block_of(block, carry):
-            for k in range(owned):
-                total = None
-                for z in range(nz * depth):
-                    where_z = me_z * depth + z if z < depth else (1 - me_z) * depth + z - depth
-                    wave = block * owned + k
-                    term = cos_ref[wave, where_z] * ones[z] + sin_ref[wave, where_z] * twos[z]
-                    total = term if total is None else total + term
-                D[c, block, k] = total
-            return carry
-
-        lax.fori_loop(0, nx, block_of, 0)
-        x_copies.append([
-            remote(D.at[c, lax.rem(me_x + o, nx)], DR.at[c, o - 1], xs.at[c, o - 1], xr.at[c, o - 1], peers_x[o - 1])
-            for o in range(1, nx)
-        ])
-        for copy in reversed(x_copies[c]):
-            copy.start()
-
-    def sum_x(c):
-        for copy in x_copies[c]:
-            copy.wait()
-        total = D[c, me_x]
-        for o in range(1, nx):
-            total = total + DR[c, o - 1]
-        E[c, me_y] = total
-        y_copies.append([
-            remote(E.at[c, me_y], E.at[c, me_y], ys.at[c, o - 1], yr.at[c, o - 1], peers_y[o - 1])
-            for o in range(1, ny)
-        ])
-        for copy in y_copies[c]:
-            copy.start()
-
-    def sum_y(c):
-        for copy in y_copies[c]:
-            copy.wait()
-        total = E[c, 0]
-        for o in range(1, ny):
-            total = total + E[c, o]
-        F[c, me_z] = total * jnp.where(cosine_lane, scale, -scale)
-        shares.append(remote(F.at[c, me_z], F.at[c, me_z], fs.at[c], fr.at[c], twin))
-        shares[c].start()
-
-    transform(0)
-    transform(1)
-    waves(0)
-    transform(2)
-    waves(1)
-    waves(2)
-    sum_x(0)
-    sum_x(1)
-    sum_y(0)
-    sum_x(2)
-    sum_y(1)
-    sum_y(2)
-    for c in range(3):
-        shares[c].wait()
-        out_ref[:, :, c] = F[c]
-
-
-def modes(spin_mid, spin_end):
-    depth, wide, lanes = spin_mid.shape[1:]
-    sizes = nx, ny, nz = (lax.axis_size("gx"), lax.axis_size("gy"), lax.axis_size("gz"))
-    total_z = depth * nz
-    owned = total_z // nx
-    half = KX // nz
-    f32 = jnp.float32
-    x_cos, x_sin = phase_table(KX, wide * nx)
-    y_cos, y_sin = phase_table(KY, lanes * ny)
-    z_cos, z_sin = phase_table(total_z, total_z)
-    x_full = np.concatenate([x_cos, x_sin], 1).reshape(nx, wide, 2 * KX).transpose(0, 2, 1)
-    y_pair = np.stack([
-        np.concatenate([y_cos, y_sin], 1).reshape(ny, lanes, 2 * KY),
-        np.concatenate([-y_sin, y_cos], 1).reshape(ny, lanes, 2 * KY),
-    ], 1).reshape(ny, 2 * lanes, 2 * KY)
-    y_full = np.zeros((ny, 4 * lanes, 4 * KY), np.float32)
-    y_full[:, : 2 * lanes, : 2 * KY] = y_pair
-    y_full[:, 2 * lanes :, 2 * KY :] = y_pair
-    scale = float(wide * nx * lanes * ny * total_z) ** -0.5
-    vmem = pl.BlockSpec(memory_space=pltpu.VMEM)
-    smem = pl.BlockSpec(memory_space=pltpu.SMEM)
-    hbm = pl.BlockSpec(memory_space=pltpu.HBM)
-    V, DMA = pltpu.VMEM, pltpu.SemaphoreType.DMA
-    width = 4 * KY
-    out = pl.pallas_call(
-        functools.partial(modes_kernel, sizes, scale),
-        out_shape=jax.ShapeDtypeStruct((nz, owned, 3, half, width), f32),
-        in_specs=[vmem, vmem, hbm, hbm, smem, smem],
-        out_specs=vmem,
-        scratch_shapes=[
-            V((2 * KX, wide), f32), V((4 * lanes, width), f32),
-            V((depth * KX, 4 * lanes), f32), V((nz, 3, depth, half, width), f32),
-            V((3, depth, half, width), f32), V((3, nx, owned, half, width), f32),
-            V((3, nx - 1, owned, half, width), f32), V((3, ny, owned, half, width), f32),
-            V((3, nz, owned, half, width), f32),
-            DMA((3,)), DMA((3,)), DMA((3, nx - 1)), DMA((3, nx - 1)), DMA((3, ny - 1)), DMA((3, ny - 1)),
-            DMA((3,)), DMA((3,)), DMA((2,)),
-        ],
-        compiler_params=pltpu.CompilerParams(collective_id=1, has_side_effects=True, vmem_limit_bytes=32 * 1024 * 1024),
-        name="modes",
-    )(spin_mid, spin_end, jnp.asarray(x_full), jnp.asarray(y_full), jnp.asarray(z_cos.T), jnp.asarray(z_sin.T))
-    out = out.reshape(nz, owned, 3, half, 2, 2, KY).transpose(4, 1, 5, 2, 0, 3, 6)
-    return out.reshape(2, owned, -1)
-
-
-def body(polar_angle, azimuth, classes, exchange_table):
-    spin_mid, spin_end = evolve(polar_angle, azimuth, classes, exchange_table)
-    both = modes(spin_mid, spin_end)
-    return (spin_end, both[0], both[1])
+    )(polar_angle, azimuth, classes, *wave_tables(depth, wide, lanes, nx, ny, nz), exchange_table)
 
 
 def solution(mesh):
     return jax.shard_map(
-        body,
+        evolve,
         mesh=mesh,
         in_specs=(
             P("gz", ("groups", "gx"), "gy"),

time: 60.5 us -> 51.5 us (0.85)
  Pallas kernels: 53.6 us -> 47.3 us
  local copies, waits for them, and re-layouts: 6 us -> 3.42 us
    pallas_call x2 -> x1, Pallas kernels: 53.6 us -> 47.3 us  [evolve(): pl.pallas_call(functools.partial(evolve_kernel, sizes), out_shape=(jax.Sh...]
    squeeze x2 -> x0, local copies, waits for them, and re-layouts: 1.7 us -> none  [body(): return (spin_end, both[0], both[1])]
    reshape x1 -> x0, local copies, waits for them, and re-layouts: 0.63 us -> none  [modes(): out.reshape(nz, owned, 3, half, 2, 2, KY).transpose(4, 1, 5, 2, 0, 3, 6)]
    unnamed x15 -> x7, local copies, waits for them, and re-layouts: 3.17 us -> 3.42 us
where the time goes in v2:
time: 51.5 us; the launch traced here: 51.4 us
  Pallas kernels  47.3 us (92%)
  local copies, waits for them, and re-layouts  3.42 us (7%)
  between operations  0.66 us (1%)
    pallas_call x1, Pallas kernels, evolve(): pl.pallas_call(functools.partial(evolve_kernel, sizes), out_shape=(jax.Sh...  47.3 us
    unnamed x7, local copies, waits for them, and re-layouts  3.42 us

profile of v2, /device:TPU:0, one launch (start us, length us, event | category | flops | bytes accessed | tf_op | source)
XLA Modules:
  0.0 51.4 jit_solution(15210567923626624189)
XLA Ops:
  0.6 47.3 %evolve.1 = (f32[3,8,64,128]{3,2,1,0:T(8,128)}, f32[4,6144]{1,0:T(4,128)}, f32[4,6144]{1,0:T(4,128)}) custom-call(f32[8,64,128]{2,1,0:T(8,128)} %polar_in.1, f32[8,64,128]{2,1,0:T(8,128)} %azimuth_in.1, s32[6,8,64,128]{3,2,1,0:T(8,128)} %classes_in.1, bf16[2,256,256]{2,1,0:T(8,128)(2,1)} %constant.6.clone.y_in, bf16[4,64,256]{2,1,0:T(8,128)(2,1)} %constant.7.clone.x_in, ...), custom_call_target="tpu_custom_call" | custom-call | tf_op jit(solution)/shard_map/evolve/pallas_call | solution.py:535
  48.0 0.0 copy-start.1
  48.0 0.0 copy-start
  48.0 2.1 %copy.13 = f32[3,8,64,128]{3,2,1,0:T(8,128)} copy(f32[3,8,64,128]{3,2,1,0:T(8,128)} %get-tuple-element.6) | data formatting | bytes 1572864
  50.1 0.0 copy-done.1
  50.1 0.6 %copy.14 = f32[4,6144]{1,0:T(4,128)} copy(f32[4,6144]{1,0:T(4,128)S(1)} %copy-done.1) | data formatting | bytes 196608
  50.8 0.0 copy-done
  50.8 0.6 %copy.15 = f32[4,6144]{1,0:T(4,128)} copy(f32[4,6144]{1,0:T(4,128)S(1)} %copy-done) | data formatting | bytes 196608
Async XLA Ops:
  48.0 2.1 %copy-start.1 = (f32[4,6144]{1,0:T(4,128)S(1)}, f32[4,6144]{1,0:T(4,128)}, u32[]{:S(2)}) copy-start(f32[4,6144]{1,0:T(4,128)} %get-tuple-element.7) | copy-start | bytes 294916
  48.0 2.8 %copy-start = (f32[4,6144]{1,0:T(4,128)S(1)}, f32[4,6144]{1,0:T(4,128)}, u32[]{:S(2)}) copy-start(f32[4,6144]{1,0:T(4,128)} %get-tuple-element.8) | copy-start | bytes 294916

commit v3 on v2

--- a/solution.py
+++ b/solution.py
@@ -56,9 +56,9 @@
 
 def evolve_kernel(sizes, polar_in, azimuth_in, classes_in, y_in, x_in, z_in, table_ref, end_ref, mid_out, end_out,
                   polar_ref, azimuth_ref, classes_ref, S, Q, J, GS, GQ, GJ, OS, OQ, OJ,
-                  low, high, lowk, highk, pack, left_pack, right_pack, out,
+                  low, high, lowk, highk, pack, left_pack, right_pack,
                   y_table, x_table, z_table, along_y, waves_xy, planes, twin_planes, sums, peer_sums, rows_sum, whole,
-                  xs, xr, ys, yr, zs, zr, gs, gr, osem, isem, ts, tr, ps, pr, qs, qr, fs, fr):
+                  xs, xr, ys, yr, zs, zr, gs, gr, isem, ts, tr, ps, pr, qs, qr, fs, fr):
     nx, ny, nz = sizes
     depth, wide, lanes = polar_ref.shape
     ext = wide + 2 * HALO
@@ -465,12 +465,10 @@
     def scaled(z, carry):
         for c in range(3):
             for r in range(inner):
-                out[c, z, pl.ds(8 * r, 8), :] = S[c, z + 1, pl.ds(HALO + 8 * r, 8), :] * (1.0 / damping)
+                end_ref[c, z, pl.ds(8 * r, 8), :] = S[c, z + 1, pl.ds(HALO + 8 * r, 8), :] * (1.0 / damping)
         return carry
 
     lax.fori_loop(0, depth, scaled, 0)
-    final = pltpu.make_async_copy(out, end_ref, osem.at[0])
-    final.start()
     wave_part(1)
     x_part(0)
     y_part(0)
@@ -478,7 +476,15 @@
     x_part(1)
     y_part(1)
     last_part(1, end_out)
-    final.wait()
+
+
+def write_kernel(*refs):
+    count = (len(refs) - 1) // 2
+    copies = [pltpu.make_async_copy(refs[i], refs[count + i], refs[-1].at[i]) for i in range(count)]
+    for copy in copies:
+        copy.start()
+    for copy in copies:
+        copy.wait()
 
 
 def phase_table(wave_count, total_length):
@@ -532,11 +538,12 @@
     V = pltpu.VMEM
     D = pltpu.SemaphoreType.DMA
     modes = jax.ShapeDtypeStruct((owned, 6 * KX * KY), f32)
-    return pl.pallas_call(
+    shapes = (jax.ShapeDtypeStruct((3, depth, wide, lanes), f32), modes, modes)
+    results = pl.pallas_call(
         functools.partial(evolve_kernel, sizes),
-        out_shape=(jax.ShapeDtypeStruct((3, depth, wide, lanes), f32), modes, modes),
+        out_shape=shapes,
         in_specs=[hbm] * 6 + [pl.BlockSpec(memory_space=pltpu.SMEM)],
-        out_specs=(anywhere, vmem, vmem),
+        out_specs=(vmem, vmem, vmem),
         scratch_shapes=[
             V((depth, wide, lanes), f32), V((depth, wide, lanes), f32), V((5, depth, wide, lanes), i32),
             V((3, depth + 2, ext, lanes), f32), V((3, depth + 2, ext, lanes), f32),
@@ -546,19 +553,26 @@
             V((2, depth, HALO, lanes), f32), V((2, depth, HALO, lanes), f32),
             V((4, depth, HALO, lanes), i32), V((4, depth, HALO, lanes), i32),
             V((5, wide, lanes), f32), V((5, ext, lanes), f32), V((5, ext, lanes), f32),
-            V((3, depth, wide, lanes), f32),
             V((2 * lanes, 2 * lanes), b16), V((2 * KX, 4 * wide), b16), V((nx * 8, 8 * nz * depth), b16),
             V((depth * wide, 2 * lanes), b16), V((depth * KX, lanes), f32),
             V((2, nz, 3, 2 * depth, half * KY), f32), V((2, 3, 2 * depth, half * KY), f32),
             V((2, 3, nx, 8, half * KY), f32), V((2, 3, nx - 1, 8, half * KY), f32),
             V((2, 3, ny, 8, half * KY), f32), V((2, 3, nz, 8, half * KY), f32),
-            D((8,)), D((8,)), D((6,)), D((6,)), D((4,)), D((4,)), D((3,)), D((3,)), D((1,)), D((8,)),
+            D((8,)), D((8,)), D((6,)), D((6,)), D((4,)), D((4,)), D((3,)), D((3,)), D((8,)),
             D((2, 3)), D((2, 3)), D((2, 3, nx - 1)), D((2, 3, nx - 1)), D((2, 3, ny - 1)), D((2, 3, ny - 1)),
             D((2, 3)), D((2, 3)),
         ],
         compiler_params=pltpu.CompilerParams(collective_id=0, has_side_effects=True, vmem_limit_bytes=60000000),
         name="evolve",
     )(polar_angle, azimuth, classes, *wave_tables(depth, wide, lanes, nx, ny, nz), exchange_table)
+    return pl.pallas_call(
+        write_kernel,
+        out_shape=shapes,
+        in_specs=[vmem] * 3,
+        out_specs=(anywhere,) * 3,
+        scratch_shapes=[D((3,))],
+        name="write",
+    )(*results)
 
 
 def solution(mesh):

time: 51.5 us -> 50.5 us (0.981)
  local copies, waits for them, and re-layouts: 3.42 us -> 0 us
  Pallas kernels: 47.3 us -> 49.7 us
    unnamed x7 -> x0, local copies, waits for them, and re-layouts: 3.42 us -> none
    pallas_call x1 -> x2, Pallas kernels: 47.3 us -> 49.7 us  [the longest x1 47.6 us: evolve(): pl.pallas_call(functools.partial(evolve_kernel, sizes), out_shape=shapes,...]
where the time goes in v3:
time: 50.5 us; the launch traced here: 50.4 us
  Pallas kernels  49.7 us (98%)
  between operations  0.64 us (1%)
    pallas_call x1, Pallas kernels, evolve(): pl.pallas_call(functools.partial(evolve_kernel, sizes), out_shape=shapes,...  47.6 us
    pallas_call x1, Pallas kernels, evolve(): pl.pallas_call(write_kernel, out_shape=shapes, in_specs=[vmem] * 3, out_s...  2.15 us

profile of v3, /device:TPU:0, one launch (start us, length us, event | category | flops | bytes accessed | tf_op | source)
XLA Modules:
  0.0 50.4 jit_solution(10305445444746836382)
XLA Ops:
  0.6 47.6 %evolve.1 = (f32[3,8,64,128]{3,2,1,0:T(8,128)}, f32[4,6144]{1,0:T(4,128)}, f32[4,6144]{1,0:T(4,128)}) custom-call(f32[8,64,128]{2,1,0:T(8,128)} %polar_in.1, f32[8,64,128]{2,1,0:T(8,128)} %azimuth_in.1, s32[6,8,64,128]{3,2,1,0:T(8,128)} %classes_in.1, bf16[2,256,256]{2,1,0:T(8,128)(2,1)} %constant.6.clone.y_in, bf16[4,64,256]{2,1,0:T(8,128)(2,1)} %constant.7.clone.x_in, ...), custom_call_target="tpu_custom_call" | custom-call | tf_op jit(solution)/shard_map/evolve/pallas_call | solution.py:542
  48.2 2.2 %write.1 = (f32[3,8,64,128]{3,2,1,0:T(8,128)}, f32[4,6144]{1,0:T(4,128)}, f32[4,6144]{1,0:T(4,128)}) custom-call(f32[3,8,64,128]{3,2,1,0:T(8,128)} %get-tuple-element.6.refs_0_, f32[4,6144]{1,0:T(4,128)} %get-tuple-element.7.refs_1_, f32[4,6144]{1,0:T(4,128)} %get-tuple-element.8.refs_2_), custom_call_target="tpu_custom_call" | custom-call | tf_op jit(solution)/shard_map/write/pallas_call | solution.py:568

commit v4 on v3

--- a/solution.py
+++ b/solution.py
@@ -54,10 +54,10 @@
     return s1 * w2 - s2 * w1, s2 * w0 - s0 * w2, s0 * w1 - s1 * w0
 
 
-def evolve_kernel(sizes, polar_in, azimuth_in, classes_in, y_in, x_in, z_in, table_ref, end_ref, mid_out, end_out,
+def evolve_kernel(sizes, polar_in, azimuth_in, classes_in, y_in, x_in, z_in, spread_in, table_ref, end_ref, mid_out, end_out,
                   polar_ref, azimuth_ref, classes_ref, S, Q, J, GS, GQ, GJ, OS, OQ, OJ,
                   low, high, lowk, highk, pack, left_pack, right_pack,
-                  y_table, x_table, z_table, along_y, waves_xy, planes, twin_planes, sums, peer_sums, rows_sum, whole,
+                  US, UQ, ins, spread_table, y_table, x_table, z_table, along_y, waves_xy, planes, twin_planes, sums, peer_sums, rows_sum, whole,
                   xs, xr, ys, yr, zs, zr, gs, gr, isem, ts, tr, ps, pr, qs, qr, fs, fr):
     nx, ny, nz = sizes
     depth, wide, lanes = polar_ref.shape
@@ -86,6 +86,7 @@
         pltpu.make_async_copy(y_in.at[me_y], y_table, isem.at[5]),
         pltpu.make_async_copy(x_in.at[me_x], x_table, isem.at[6]),
         pltpu.make_async_copy(z_in.at[me_z], z_table, isem.at[7]),
+        pltpu.make_async_copy(spread_in, spread_table, isem.at[8]),
     ]
     for copy in fetches + tables:
         copy.start()
@@ -101,6 +102,13 @@
         return pltpu.make_async_remote_copy(
             src_ref=src, dst_ref=dst, send_sem=send, recv_sem=recv, device_id=who, device_id_type=MESH
         )
+
+    def split(value):
+        big = value.astype(jnp.bfloat16)
+        return big, (value - big.astype(jnp.float32)).astype(jnp.bfloat16)
+
+    def dot(a, b):
+        return jnp.dot(a, b, preferred_element_type=jnp.float32)
 
     top = pl.ds(wide - HALO, HALO)
     bottom = pl.ds(0, HALO)
@@ -197,6 +205,13 @@
             remote(field.at[:, depth], field.at[:, 0], zs.at[base + 1], zr.at[base + 1], z_up),
         ]
 
+    def spread(G, U):
+        big, small = split(G[...].reshape(3 * ext, lanes))
+        both = jnp.concatenate([big, small], 1)
+        for k in range(depth // 2):
+            cols = pl.ds(2 * lanes * k, 2 * lanes)
+            U[:, :, cols] = dot(both, spread_table[:, cols]).reshape(3, ext, 2 * lanes)
+
     def g_copy(ghost, other, base):
         return remote(ghost, other, gs.at[base], gr.at[base], z_up)
 
@@ -223,6 +238,9 @@
     lax.fori_loop(0, tiles, ghosts, 0)
     g_copy(GS, OS, 0).start()
     g_copy(GJ.at[2], OJ, 2).start()
+    for copy in tables:
+        copy.wait()
+    spread(GS, US)
 
     def corners(z, carry):
         for row in (0, HALO + wide):
@@ -238,49 +256,52 @@
         behind = ref[pl.ds(8 * r - 1, 8), :] if r > 0 else pltpu.roll(value, 1, 0)
         return ahead, behind
 
-    def plane(F, G, z, finish, rows_of):
-        up_shift = lanes - (group * z + HALO)
-        for r in rows_of:
-            rows = pl.ds(8 * r, 8)
-            c0, c1, c2, c4 = (J[d, z + 1, rows, :] for d in range(4))
-            c3 = J[0, z + 1, pl.ds(8 * r - 1, 8), :] if r > 0 else pltpu.roll(c0, 1, 0)
-            c5 = J[2, z, rows, :]
-            spin, field = [], []
-            for c in range(3):
-                M = F[c, z + 1, rows, :]
-                ahead, behind = x_pair(F.at[c, z + 1], r, M)
-                U = pltpu.roll(G[c, rows, :], up_shift, 1)
-                right = jnp.where(lane == lanes - 1, U, pltpu.roll(M, lanes - 1, 1))
-                left = jnp.where(lane == 0, U, pltpu.roll(M, 1, 1))
-                total = (c0 * ahead + c3 * behind) + (c2 * F[c, z + 2, rows, :] + c5 * F[c, z, rows, :])
-                total = total + (c1 * right + c4 * left)
-                spin.append(M)
-                field.append(total)
-            finish(spin, descent(spin, field), z, rows)
-
-    def ghost_pass(F, G, other, finish):
-        for r in range(tiles):
-            rows = pl.ds(8 * r, 8)
-            c0, c1, c2, c4 = (GJ[d, rows, :] for d in range(4))
-            c3 = GJ[0, pl.ds(8 * r - 1, 8), :] if r > 0 else pltpu.roll(c0, 1, 0)
-            c5 = pltpu.roll(jnp.where(lane < lanes - group, c2, OJ[rows, :]), group, 1)
-            spin, field = [], []
-            for c in range(3):
-                M = G[c, rows, :]
-                O = other[c, rows, :]
-                I = M
-                for z in range(depth):
-                    I = jnp.where(group_of == z, pltpu.roll(F[c, z + 1, rows, :], group * z + HALO, 1), I)
-                ahead, behind = x_pair(G.at[c], r, M)
-                right = jnp.where(place == HALO, I, pltpu.roll(M, 1, 1))
-                left = jnp.where(place == HALO - 1, I, pltpu.roll(M, lanes - 1, 1))
-                above = pltpu.roll(jnp.where(lane >= group, M, O), lanes - group, 1)
-                below = pltpu.roll(jnp.where(lane < lanes - group, M, O), group, 1)
-                total = (c0 * ahead + c3 * behind) + (c2 * above + c5 * below)
-                total = total + (c1 * right + c4 * left)
-                spin.append(M)
-                field.append(total)
-            finish(spin, descent(spin, field), rows)
+    def plane_tile(F, U_ref, z, finish, r):
+        rows = pl.ds(8 * r, 8)
+        c0, c1, c2, c4 = (J[d, z + 1, rows, :] for d in range(4))
+        c3 = J[0, z + 1, pl.ds(8 * r - 1, 8), :] if r > 0 else pltpu.roll(c0, 1, 0)
+        c5 = J[2, z, rows, :]
+        spin, field = [], []
+        for c in range(3):
+            M = F[c, z + 1, rows, :]
+            ahead, behind = x_pair(F.at[c, z + 1], r, M)
+            U = U_ref[c, rows, pl.ds(z * lanes, lanes)]
+            right = jnp.where(lane == lanes - 1, U, pltpu.roll(M, lanes - 1, 1))
+            left = jnp.where(lane == 0, U, pltpu.roll(M, 1, 1))
+            total = (c0 * ahead + c3 * behind) + (c2 * F[c, z + 2, rows, :] + c5 * F[c, z, rows, :])
+            total = total + (c1 * right + c4 * left)
+            spin.append(M)
+            field.append(total)
+        finish(spin, descent(spin, field), z, rows)
+
+    def collect(F, r):
+        rows = pl.ds(8 * r, 8)
+        for c in range(3):
+            I = pltpu.roll(F[c, 1, rows, :], HALO, 1)
+            for z in range(1, depth):
+                I = jnp.where(group_of == z, pltpu.roll(F[c, z + 1, rows, :], group * z + HALO, 1), I)
+            ins[c, rows, :] = I
+
+    def ghost_tile(G, other, finish, r):
+        rows = pl.ds(8 * r, 8)
+        c0, c1, c2, c4 = (GJ[d, rows, :] for d in range(4))
+        c3 = GJ[0, pl.ds(8 * r - 1, 8), :] if r > 0 else pltpu.roll(c0, 1, 0)
+        c5 = pltpu.roll(jnp.where(lane < lanes - group, c2, OJ[rows, :]), group, 1)
+        spin, field = [], []
+        for c in range(3):
+            M = G[c, rows, :]
+            O = other[c, rows, :]
+            I = ins[c, rows, :]
+            ahead, behind = x_pair(G.at[c], r, M)
+            right = jnp.where(place == HALO, I, pltpu.roll(M, 1, 1))
+            left = jnp.where(place == HALO - 1, I, pltpu.roll(M, lanes - 1, 1))
+            above = pltpu.roll(jnp.where(lane >= group, M, O), lanes - group, 1)
+            below = pltpu.roll(jnp.where(lane < lanes - group, M, O), group, 1)
+            total = (c0 * ahead + c3 * behind) + (c2 * above + c5 * below)
+            total = total + (c1 * right + c4 * left)
+            spin.append(M)
+            field.append(total)
+        finish(spin, descent(spin, field), rows)
 
     def predict(spin, change, z, rows):
         for c in range(3):
@@ -298,32 +319,25 @@
         for c in range(3):
             GS[c, rows, :] = 0.5 * (GS[c, rows, :] + (spin[c] - change[c]))
 
-    def stage(F, G, O, base, finish, finish_ghost, send_main, send_ghost, first=None, every=range(tiles)):
-        def inside(i, carry):
-            plane(F, G, 2 * i + 1, finish, every)
-            plane(F, G, 2 * i + 2, finish, every)
-            return carry
-
-        lax.fori_loop(0, (depth - 2) // 2, inside, 0)
+    def stage(F, G, O, U, base, finish, finish_ghost, send_main, send_ghost, first=None, every=range(tiles)):
+        for r in every:
+            if finish_ghost is not None:
+                collect(F, r)
+            for z in range(1, depth - 1):
+                plane_tile(F, U, z, finish, r)
         for copy in z_copies(F, 2 * base):
             copy.wait()
-        plane(F, G, 0, finish, every)
-        plane(F, G, depth - 1, finish, every)
+        for r in every:
+            for z in (0, depth - 1):
+                plane_tile(F, U, z, finish, r)
         send_main()
         g_copy(G, O, base).wait()
-        if finish_ghost is None:
-            return
         if first is not None:
             first()
-        ghost_pass(F, G, O, finish_ghost)
-        send_ghost()
-
-    def split(value):
-        big = value.astype(jnp.bfloat16)
-        return big, (value - big.astype(jnp.float32)).astype(jnp.bfloat16)
-
-    def dot(a, b):
-        return jnp.dot(a, b, preferred_element_type=jnp.float32)
+        if finish_ghost is not None:
+            for r in every:
+                ghost_tile(G, O, finish_ghost, r)
+            send_ghost()
 
     half = KX // nz
     quad = lanes // KY
@@ -434,7 +448,11 @@
             copy.start()
 
     def predict_stage(first=None):
-        stage(S, GS, OS, 0, predict, predict_ghost, send_q, lambda: g_copy(GQ, OQ, 1).start(), first)
+        def send_ghost():
+            g_copy(GQ, OQ, 1).start()
+            spread(GQ, UQ)
+
+        stage(S, GS, OS, US, 0, predict, predict_ghost, send_q, send_ghost, first)
 
     def step(turn, carry):
         def couplings():
@@ -442,8 +460,12 @@
             def _():
                 g_copy(GJ.at[2], OJ, 2).wait()
 
+        def send_ghost():
+            g_copy(GS, OS, 0).start()
+            spread(GS, US)
+
         predict_stage(couplings)
-        stage(Q, GQ, OQ, 1, correct, correct_ghost, send_s, lambda: g_copy(GS, OS, 0).start())
+        stage(Q, GQ, OQ, UQ, 1, correct, correct_ghost, send_s, send_ghost)
 
         @pl.when(turn == STEPS // 2 - 1)
         def _():
@@ -455,11 +477,9 @@
 
         return carry
 
-    for copy in tables:
-        copy.wait()
     lax.fori_loop(0, STEPS - 1, step, 0)
     predict_stage()
-    stage(Q, GQ, OQ, 1, correct, None, lambda: None, None, every=range(1, tiles - 1))
+    stage(Q, GQ, OQ, UQ, 1, correct, None, lambda: None, None, every=range(1, tiles - 1))
     local_part(1)
 
     def scaled(z, carry):
@@ -521,7 +541,12 @@
                     z_full[first, :, p * owned : (p + 1) * owned, place, part] = values
     big, small = halves(z_full.reshape(nz, nx * 8, nz * 2 * depth))
     z_all = np.concatenate([big, big, small, small], 2)
-    return jnp.asarray(y_all), jnp.asarray(x_all), jnp.asarray(z_all)
+    spread = np.zeros((2, lanes, depth, lanes))
+    for z in range(depth):
+        spread[:, 2 * HALO * z + HALO, z, 0] = 1.0
+        spread[:, 2 * HALO * z + HALO - 1, z, lanes - 1] = 1.0
+    spread_all = spread.reshape(2 * lanes, depth * lanes).astype(jnp.bfloat16)
+    return jnp.asarray(y_all), jnp.asarray(x_all), jnp.asarray(z_all), jnp.asarray(spread_all)
 
 
 def evolve(polar_angle, azimuth, classes, exchange_table):
@@ -542,7 +567,7 @@
     results = pl.pallas_call(
         functools.partial(evolve_kernel, sizes),
         out_shape=shapes,
-        in_specs=[hbm] * 6 + [pl.BlockSpec(memory_space=pltpu.SMEM)],
+        in_specs=[hbm] * 7 + [pl.BlockSpec(memory_space=pltpu.SMEM)],
         out_specs=(vmem, vmem, vmem),
         scratch_shapes=[
             V((depth, wide, lanes), f32), V((depth, wide, lanes), f32), V((5, depth, wide, lanes), i32),
@@ -553,12 +578,14 @@
             V((2, depth, HALO, lanes), f32), V((2, depth, HALO, lanes), f32),
             V((4, depth, HALO, lanes), i32), V((4, depth, HALO, lanes), i32),
             V((5, wide, lanes), f32), V((5, ext, lanes), f32), V((5, ext, lanes), f32),
+            V((3, ext, depth * lanes), f32), V((3, ext, depth * lanes), f32), V((3, ext, lanes), f32),
+            V((2 * lanes, depth * lanes), b16),
             V((2 * lanes, 2 * lanes), b16), V((2 * KX, 4 * wide), b16), V((nx * 8, 8 * nz * depth), b16),
             V((depth * wide, 2 * lanes), b16), V((depth * KX, lanes), f32),
             V((2, nz, 3, 2 * depth, half * KY), f32), V((2, 3, 2 * depth, half * KY), f32),
             V((2, 3, nx, 8, half * KY), f32), V((2, 3, nx - 1, 8, half * KY), f32),
             V((2, 3, ny, 8, half * KY), f32), V((2, 3, nz, 8, half * KY), f32),
-            D((8,)), D((8,)), D((6,)), D((6,)), D((4,)), D((4,)), D((3,)), D((3,)), D((8,)),
+            D((8,)), D((8,)), D((6,)), D((6,)), D((4,)), D((4,)), D((3,)), D((3,)), D((9,)),
             D((2, 3)), D((2, 3)), D((2, 3, nx - 1)), D((2, 3, nx - 1)), D((2, 3, ny - 1)), D((2, 3, ny - 1)),
             D((2, 3)), D((2, 3)),
         ],

time: 50.5 us -> 50.1 us (level)
  no operation moved by 1% of the time
where the time goes in v4:
time: 50.1 us; the launch traced here: 49.9 us
  Pallas kernels  49.3 us (98%)
  between operations  0.64 us (1%)
    pallas_call x1, Pallas kernels, evolve(): pl.pallas_call(functools.partial(evolve_kernel, sizes), out_shape=shapes,...  47.1 us
    pallas_call x1, Pallas kernels, evolve(): pl.pallas_call(write_kernel, out_shape=shapes, in_specs=[vmem] * 3, out_s...  2.15 us

profile of v4, /device:TPU:0, one launch (start us, length us, event | category | flops | bytes accessed | tf_op | source)
XLA Modules:
  0.0 49.9 jit_solution(16902875913174335119)
XLA Ops:
  0.6 47.1 %evolve.1 = (f32[3,8,64,128]{3,2,1,0:T(8,128)}, f32[4,6144]{1,0:T(4,128)}, f32[4,6144]{1,0:T(4,128)}) custom-call(f32[8,64,128]{2,1,0:T(8,128)} %polar_in.1, f32[8,64,128]{2,1,0:T(8,128)} %azimuth_in.1, s32[6,8,64,128]{3,2,1,0:T(8,128)} %classes_in.1, bf16[2,256,256]{2,1,0:T(8,128)(2,1)} %constant.8.clone.y_in, bf16[4,64,256]{2,1,0:T(8,128)(2,1)} %constant.9.clone.x_in, ...), custom_call_target="tpu_custom_call" | custom-call | tf_op jit(solution)/shard_map/evolve/pallas_call | solution.py:567
  47.8 2.2 %write.1 = (f32[3,8,64,128]{3,2,1,0:T(8,128)}, f32[4,6144]{1,0:T(4,128)}, f32[4,6144]{1,0:T(4,128)}) custom-call(f32[3,8,64,128]{3,2,1,0:T(8,128)} %get-tuple-element.6.refs_0_, f32[4,6144]{1,0:T(4,128)} %get-tuple-element.7.refs_1_, f32[4,6144]{1,0:T(4,128)} %get-tuple-element.8.refs_2_), custom_call_target="tpu_custom_call" | custom-call | tf_op jit(solution)/shard_map/write/pallas_call | solution.py:595
